TPU v7x, 256 devices: a whole 4x4x8 slice. The times are simulated.
256 devices in a mesh: gx: 32 (over y, z_lo, core), gy: 8 (over z_hi, x).
Axes of the slice: x: 4, y: 4, z: 8 (z_hi: 2, z_lo: 4; z = z_hi * 4 + z_lo), core: 2. Of those that a mesh axis runs over, the one named last changes fastest.
Arguments:
- features: bfloat16 [32, 8, 3, 512, 192], P('gx', 'gy'), may hold values from -6 to 6
- weight: bfloat16 [5184, 192], replicated, may hold values from -0.078125 to 0.078125
- cotangent: bfloat16 [32, 8, 3, 64, 192], P('gx', 'gy'), may hold values from -6 to 6
- valid: int32 [32, 8, 3], P('gx', 'gy'), may hold values from 0 to 1, as said below
- local_rules: int32 [32, 8, 2, 12], P('gx', 'gy'), may hold values from 0 to 3, as said below
- local_codes: int32 [32, 8, 12], P('gx', 'gy'), may hold values from 0 to 7
- remote_rules: int32 [32, 8, 2, 3, 3], P('gx', 'gy'), may hold values from 0 to 3, as said below
- remote_codes: int32 [32, 8, 3, 3], P('gx', 'gy'), may hold values from 1 to 7, as said below
Outputs:
- output: bfloat16 [32, 8, 3, 64, 192], P('gx', 'gy')
- features_grad: bfloat16 [32, 8, 3, 512, 192], P('gx', 'gy')
- weight_grad: float32 [5184, 192], P('gx')
Inputs may be any that keep to these rules, and one draw needn't show every extreme that they name: `valid`: 1 marks a live brick slot; on each device the live slots come first and at least one slot is live. `local_rules`: entry [., ., 0, e] is a source slot and [., ., 1, e] a target slot of the same device; a target 3 marks an empty entry; non-empty entries name live slots. `remote_rules`: class m (third dimension) entry: a source slot on this device and a target slot on the device one step higher along gx (m = 0), along gy (m = 1) or along both (m = 2); a target 3 marks an empty entry; non-empty entries name live slots; devices at the upper end of an axis have no non-empty entries in the classes that cross it. `remote_codes`: the offset k mod 2 is 1 in classes 0 and 2, and the offset (k // 2) mod 2 is 1 in classes 1 and 2.
All inputs are finite; a program needn't handle non-finite values.
Results may differ from a plain program's by a relative error of at most 0.0045.
Values may be sent and summed in bfloat16 or wider, within the bound.
No kernel may reach another device: no remote copies, remote signals or barrier semaphores. Data moves between devices by JAX's collectives and lax.ppermute only.
A program may use at most 128 MiB of HBM per device.

v0:
```python
import functools

import jax
import jax.numpy as jnp
from jax import lax
from jax.experimental import pallas as pl
from jax.experimental.pallas import tpu as pltpu
from jax.sharding import PartitionSpec as P


INTERPRET = False
BF = jnp.bfloat16
F32 = jnp.float32
VM = pltpu.MemorySpace.VMEM
HB = pltpu.MemorySpace.HBM
TABLES = ((1, 1, 2, 12), (1, 1, 12), (1, 1, 3, 2, 3), (1, 3, 1, 3))
FLAGS = ((1, 1, 3),)

PARITY = (1, 0, 1)
SHIFT = (1, 0, 0)
TAPS = [(e, f, g) for e in range(3) for f in range(3) for g in range(3)]


def tap_parity(tap):
    return PARITY[tap[0]] * 4 + PARITY[tap[1]] * 2 + PARITY[tap[2]]


def tap_shift(tap):
    return SHIFT[tap[0]] + 2 * SHIFT[tap[1]] + 4 * SHIFT[tap[2]]


def call(kernel, outs, args, spaces, scratch, flops, limit=4):
    nbytes = sum(a.size * a.dtype.itemsize for a in args)
    if not INTERPRET:
        args = [
            pltpu.with_memory_space_constraint(a, HB) if s == HB else a
            for a, s in zip(args, spaces)
        ]
    return pl.pallas_call(
        kernel,
        out_shape=outs,
        in_specs=[pl.BlockSpec(memory_space=s) for s in spaces],
        out_specs=jax.tree.map(lambda _: pl.BlockSpec(memory_space=VM), outs),
        scratch_shapes=scratch,
        compiler_params=pltpu.CompilerParams(vmem_limit_bytes=limit << 20),
        cost_estimate=pl.CostEstimate(flops=flops, bytes_accessed=nbytes, transcendentals=0),
        interpret=INTERPRET,
    )(*args)


def scalars(shapes):
    return [pltpu.SMEM(shape, jnp.int32) for shape in shapes] + [pltpu.SemaphoreType.DMA((8,))]


def fetch(sources, targets, sems):
    copies = [
        pltpu.make_async_copy(source, target, sems.at[n])
        for n, (source, target) in enumerate(zip(sources, targets))
    ]
    for copy in copies:
        copy.start()
    return copies


def parity_order():
    row = lax.broadcasted_iota(jnp.int32, (512, 512), 0)
    voxel = lax.broadcasted_iota(jnp.int32, (512, 512), 1)
    par, r, p, q = row >> 6, row >> 4 & 3, row >> 2 & 3, row & 3
    x = 2 * p + (par >> 2)
    y = 2 * q + (par >> 1 & 1)
    z = 2 * r + (par & 1)
    return jnp.where(voxel == x * 64 + y * 8 + z, 1.0, 0.0).astype(BF)


def split_kernel(valid_in, feat_in, out, feat, valid, sems):
    copies = fetch((valid_in, feat_in), (valid, feat), sems)
    order = parity_order()
    for copy in copies:
        copy.wait()
    for slot in range(3):
        rows = lax.dot_general(
            order, feat[0, 0, slot], (((1,), (1,)), ((), ())), preferred_element_type=F32
        )
        rows = (rows * valid[0, 0, slot].astype(F32)).astype(BF)
        for par in range(8):
            out[par, slot * 64 : slot * 64 + 64, :] = rows[par * 64 : par * 64 + 64]


def mask_kernel(valid_in, cot_in, masked, face, cot, valid, sems):
    for copy in fetch((valid_in, cot_in), (valid, cot), sems):
        copy.wait()
    for slot in range(3):
        rows = cot[0, 0, slot].astype(F32) * valid[0, 0, slot].astype(F32)
        rows = rows.astype(BF)
        masked[slot] = rows
        face[slot] = rows[0:16]


def pack_kernel(masked, cot_x, out):
    for slot in range(3):
        rows = masked[slot].astype(F32)
        edge = cot_x[slot].astype(F32)[0:4]
        face = [rows[p * 16 : p * 16 + 4] for p in range(4)]
        out[slot] = jnp.concatenate(face + [edge, jnp.zeros((12, 192), F32)], axis=0).astype(BF)


def row_ids():
    return lax.broadcasted_iota(jnp.int32, (64, 192), 0)


def gather_shift(first, second, axis):
    if axis == 2:
        return jnp.concatenate([first[16:], second[:16]], axis=0)
    step = 4 if axis == 0 else 1
    at = row_ids() // step % 4
    up = pltpu.roll(first, 64 - step, 0)
    wrap = pltpu.roll(second, 3 * step, 0)
    return jnp.where(at == 3, wrap, up)


def to_cube_order(cube, low, high):
    low[...] = cube[:, :128]
    high[:, 0:64] = cube[:, 128:]
    parts = []
    for r in range(4):
        take = pl.ds(r, 16, stride=4)
        parts.append(jnp.concatenate([low[take, :], high[take, :][:, 0:64]], axis=1))
    return jnp.concatenate(parts, axis=0)


def weight_kernel(
    lrules_in, lcodes_in, rrules_in, rcodes_in, split, masked, cot_x, cot_y,
    keep, send, shifts, cubes, grads, low, high, total, lrules, lcodes, rrules, rcodes, sems,
):
    copies = fetch(
        (lrules_in, lcodes_in, rrules_in, rcodes_in), (lrules, lcodes, rrules, rcodes), sems
    )
    zero = jnp.zeros((64, 192), F32)
    for group in range(16):
        cubes[group] = zero
    for slot in range(3):
        cubes[slot] = to_cube_order(masked[slot].astype(F32), low, high)
        from_x = cot_x[slot].astype(F32)
        from_y = cot_y[slot].astype(F32)
        for r in range(4):
            for n in range(4):
                put = slice(r * 16 + n, r * 16 + n + 1)
                cubes[4 + slot, put, :] = from_x[n * 4 + r : n * 4 + r + 1]
                put = slice(r * 16 + n * 4, r * 16 + n * 4 + 1)
                cubes[8 + slot, put, :] = from_y[n * 4 + r : n * 4 + r + 1]
            put = slice(r * 16, r * 16 + 1)
            cubes[12 + slot, put, :] = from_y[16 + r : 17 + r]
    for entry in range(32):
        grads[entry] = zero
    for copy in copies:
        copy.wait()
    for e in range(12):
        at = lrules[0, 0, 0, e] * 8 + lcodes[0, 0, e]
        grads[at] += cubes[lrules[0, 0, 1, e]]
    for m in range(3):
        for e in range(3):
            at = rrules[0, 0, m, 0, e] * 8 + rcodes[0, m, 0, e]
            grads[at] += cubes[(m + 1) * 4 + rrules[0, 0, m, 1, e]]
    for slot in range(3):
        level = {}
        for u in range(2):
            for v in range(2):
                first = grads[slot * 8 + u + 2 * v]
                second = grads[slot * 8 + u + 2 * v + 4]
                level[u, v, 0] = first
                level[u, v, 1] = gather_shift(first, second, 2)
        after = {}
        for v in range(2):
            for w in range(2):
                after[0, v, w] = level[0, v, w]
                after[1, v, w] = gather_shift(level[0, v, w], level[1, v, w], 0)
        for u in range(2):
            for w in range(2):
                rows = slice(slot * 64, slot * 64 + 64)
                shifts[u + 4 * w, rows, :] = after[u, 0, w].astype(BF)
                shifts[u + 2 + 4 * w, rows, :] = gather_shift(
                    after[u, 0, w], after[u, 1, w], 1
                ).astype(BF)
    for index, tap in enumerate(TAPS):
        total[index * 192 : (index + 1) * 192, :] = lax.dot_general(
            split[tap_parity(tap)],
            shifts[tap_shift(tap)],
            (((0,), (0,)), ((), ())),
            preferred_element_type=F32,
        )
    here = lax.axis_index("gx")
    core = here % 2
    for m in range(16):
        other = m % 4 * 4 + m // 4
        for own in range(2):
            keeper = core if own else 1 - core
            block = ((here // 2) ^ jnp.where(keeper == 0, m, other)) * 2 + keeper
            start = pl.multiple_of(block * 162 // 8 * 8, 8)
            left = total[pl.ds(start, 168), 0:128]
            right = jnp.concatenate(
                [
                    total[pl.ds(start, 88), 128:192],
                    total[pl.ds(pl.multiple_of(start + 80, 8), 88), 128:192],
                ],
                axis=1,
            )
            if own:
                keep[m * 256 : m * 256 + 168, :] = left
                keep[m * 256 + 168 : m * 256 + 256, :] = right
            else:
                send[m * 256 : m * 256 + 168, :] = left.astype(BF)
                send[m * 256 + 168 : m * 256 + 256, :] = right.astype(BF)


def scatter_shift(first, second, axis):
    step = {2: 16, 0: 4, 1: 1}[axis]
    at = row_ids() // step % 4
    down = pltpu.roll(second, step, 0)
    out = pltpu.roll(second, 64 - 3 * step, 0)
    return first + jnp.where(at == 0, 0.0, down), jnp.where(at == 0, out, 0.0)


def forward_kernel(
    lrules_in, lcodes_in, rrules_in, rcodes_in, split, weight,
    local, to_x, to_y, regions, sums, pack, lrules, lcodes, rrules, rcodes, sems,
):
    copies = fetch(
        (lrules_in, lcodes_in, rrules_in, rcodes_in), (lrules, lcodes, rrules, rcodes), sems
    )
    for shift in range(8):
        acc = None
        for index, tap in enumerate(TAPS):
            if tap_shift(tap) == shift:
                part = lax.dot_general(
                    split[tap_parity(tap)],
                    weight[:, index * 192 : (index + 1) * 192],
                    (((1,), (1,)), ((), ())),
                    preferred_element_type=F32,
                )
                acc = part if acc is None else acc + part
        for slot in range(3):
            regions[slot * 8 + shift] = acc[slot * 64 : slot * 64 + 64]
    for slot in range(3):
        for bit, axis in ((1, 0), (2, 1), (4, 2)):
            for other in range(8):
                if other & bit:
                    continue
                inner, outer = scatter_shift(
                    regions[slot * 8 + other], regions[slot * 8 + other + bit], axis
                )
                regions[slot * 8 + other] = inner
                regions[slot * 8 + other + bit] = outer
    for entry in range(16):
        sums[entry] = jnp.zeros((64, 192), F32)
    for copy in copies:
        copy.wait()
    for e in range(12):
        at = jnp.minimum(lrules[0, 0, 0, e], 2) * 8 + lcodes[0, 0, e]
        sums[lrules[0, 0, 1, e]] += regions[at]
    for m in range(3):
        for e in range(3):
            at = jnp.minimum(rrules[0, 0, m, 0, e], 2) * 8 + rcodes[0, m, 0, e]
            sums[(m + 1) * 4 + rrules[0, 0, m, 1, e]] += regions[at]
    for t in range(3):
        local[t] = sums[t]
        pack[16:32, :] = jnp.zeros((16, 192), F32)
        for r in range(4):
            pack[r * 4 : r * 4 + 4, :] = sums[4 + t, r * 16 : r * 16 + 4, :]
            pack[16 + r : 17 + r, :] = sums[12 + t, r * 16 : r * 16 + 1, :]
            for p in range(4):
                to_y[t, r * 4 + p : r * 4 + p + 1, :] = sums[
                    8 + t, r * 16 + p * 4 : r * 16 + p * 4 + 1, :
                ]
        to_x[t] = pack[...].astype(BF)


def join_kernel(to_y, got_x, out, rows):
    for t in range(3):
        edge = got_x[t].astype(F32)
        rows[...] = to_y[t]
        for r in range(4):
            rows[r * 4 : r * 4 + 1, :] += edge[16 + r : 17 + r]
        out[t] = rows[...].astype(BF)


def output_kernel(valid_in, local, got_x, got_y, out, acc, low, high, valid, sems):
    for copy in fetch((valid_in,), (valid,), sems):
        copy.wait()
    for t in range(3):
        acc[...] = local[t]
        from_x = got_x[t].astype(F32)
        from_y = got_y[t].astype(F32)
        for r in range(4):
            acc[r * 16 : r * 16 + 4, :] += from_x[r * 4 : r * 4 + 4]
        for row in range(16):
            acc[row * 4 : row * 4 + 1, :] += from_y[row : row + 1]
        live = valid[0, 0, t].astype(F32)
        for r in range(4):
            rows = acc[r * 16 : r * 16 + 16, :] * live
            put = pl.ds(r, 16, stride=4)
            low[put, :] = rows[:, 0:128]
            high[put, :] = jnp.concatenate([rows[:, 128:192], rows[:, 128:192]], axis=1)
        out[0, 0, t, :, 0:128] = low[...].astype(BF)
        out[0, 0, t, :, 128:192] = high[:, 0:64].astype(BF)


def features_kernel(valid_in, shifts, weight, out, cubes, valid, sems):
    for copy in fetch((valid_in,), (valid,), sems):
        copy.wait()
    for par in range(8):
        acc = None
        for index, tap in enumerate(TAPS):
            if tap_parity(tap) == par:
                part = jnp.dot(
                    shifts[tap_shift(tap)],
                    weight[:, index * 192 : (index + 1) * 192],
                    preferred_element_type=F32,
                )
                acc = part if acc is None else acc + part
        for slot in range(3):
            live = valid[0, 0, slot].astype(F32)
            rows = acc[slot * 64 : slot * 64 + 64] * live
            cubes[slot, par * 64 : par * 64 + 64, :] = rows.astype(BF)
    order = parity_order()
    for slot in range(3):
        out[0, 0, slot] = lax.dot_general(
            cubes[slot], order, (((0,), (0,)), ((), ())), preferred_element_type=F32
        ).astype(BF)


def share_kernel(mine, other, out, rows):
    full = mine[...].astype(F32) + other[...].astype(F32)
    rows[:, 0:128] = full[0:168]
    rows[0:88, 128:192] = full[168:256, 0:64]
    rows[88:168, 128:192] = full[176:256, 64:128]
    offset = lax.axis_index("gx") % 4 * 2
    for case in range(4):
        @pl.when(offset == case * 2)
        def _(case=case):
            out[...] = rows[case * 2 : case * 2 + 162, :]


def swap(value, axis, size, bits):
    return lax.ppermute(value, axis, [(i, i ^ bits) for i in range(size)])


def step(value, axis, sign):
    size = lax.axis_size(axis)
    route = [(i, i + sign) for i in range(size) if 0 <= i + sign < size]
    return lax.ppermute(value, axis, route)


def split_sum_kernel(count, mine, *refs):
    got, first, rest = refs[:count], refs[count], refs[count + 1 :]
    size = first.shape[0]
    for d in range(4):
        rows = slice(d * size, d * size + size)
        full = mine[rows, :]
        for ref in got:
            full = full + ref[rows, :].astype(F32)
        if d == 0:
            first[...] = full
        else:
            rest[d - 1][...] = full.astype(BF)


def split_sum(mine, got, limit):
    size = mine.shape[0] // 4
    outs = (jax.ShapeDtypeStruct((size, 128), F32),) + (jax.ShapeDtypeStruct((size, 128), BF),) * 3
    args = (mine, *got)
    kernel = functools.partial(split_sum_kernel, len(got))
    first, *rest = call(kernel, outs, args, (VM,) * len(args), [], 0, limit)
    return first, rest


def sum_kernel(first, one, two, three, out):
    total = first[...].astype(F32) + one[...].astype(F32)
    out[...] = (total + (two[...].astype(F32) + three[...].astype(F32))).astype(BF)


def sum_of(values):
    return call(sum_kernel, jax.ShapeDtypeStruct((256, 128), BF), values, (VM,) * 4, [], 0, 2)


def turns(parts, first_bits, second_bits):
    got = {}
    for d in (2, 3, 1):
        route = [(i, i ^ ((second_bits if i % 2 else first_bits) * d)) for i in range(32)]
        got[d] = lax.ppermute(parts[d - 1], "gx", route)
    return [got[1], got[2], got[3]]


def together(*values):
    return lax.optimization_barrier(values)


def shards(
    features, weight, cotangent, valid, local_rules, local_codes, remote_rules, remote_codes
):
    rules = (
        local_rules,
        local_codes,
        jnp.transpose(remote_rules, (0, 1, 3, 2, 4)),
        jnp.transpose(remote_codes, (0, 2, 1, 3)),
    )
    weight = weight.T
    features = jnp.swapaxes(features, 3, 4)
    shape = jax.ShapeDtypeStruct
    flops = 2 * 27 * 192**3
    masked, face = call(
        mask_kernel,
        (shape((3, 64, 192), BF), shape((3, 16, 192), BF)),
        (valid, cotangent),
        (HB, HB),
        [pltpu.VMEM((1, 1, 3, 64, 192), BF)] + scalars(FLAGS),
        0,
        2,
    )
    cot_x = step(face, "gx", -1)
    packed = call(pack_kernel, shape((3, 32, 192), BF), (masked, cot_x), (VM, VM), [], 0, 2)
    cot_y = step(packed, "gy", -1)
    split = call(
        split_kernel,
        shape((8, 192, 192), BF),
        (valid, together(features, packed)[0]),
        (HB, HB),
        [pltpu.VMEM((1, 1, 3, 192, 512), BF)] + scalars(FLAGS),
        0,
        6,
    )
    keep, send, shifts = call(
        weight_kernel,
        (shape((4096, 128), F32), shape((4096, 128), BF), shape((8, 192, 192), BF)),
        (*rules, split, masked, cot_x, cot_y),
        (HB,) * 4 + (VM,) * 4,
        [pltpu.VMEM((16, 64, 192), F32), pltpu.VMEM((32, 64, 192), F32)]
        + [pltpu.VMEM((64, 128), F32)] * 2
        + [pltpu.VMEM((5184, 192), F32)]
        + scalars(TABLES),
        flops,
        18,
    )
    send, split, weight = together(send, split, weight)
    arrived = swap(send, "gx", 32, 1)
    local, to_x, to_y = call(
        forward_kernel,
        (shape((3, 64, 192), F32), shape((3, 32, 192), BF), shape((3, 16, 192), F32)),
        (*rules, split, weight),
        (HB,) * 4 + (VM,) * 2,
        [pltpu.VMEM((24, 64, 192), F32), pltpu.VMEM((16, 64, 192), F32), pltpu.VMEM((32, 192), F32)]
        + scalars(TABLES),
        flops,
        12,
    )
    arrived, local, to_x, to_y = together(arrived, local, to_x, to_y)
    first, rest = split_sum(keep, [arrived], 8)
    rest, shifts, to_x = together(rest, shifts, to_x)
    arrived = turns(rest, 8, 2)
    got_x = step(to_x, "gx", 1)
    features_grad = call(
        features_kernel,
        shape((1, 1, 3, 192, 512), BF),
        (valid, shifts, weight),
        (HB, VM, VM),
        [pltpu.VMEM((3, 512, 192), BF)] + scalars(FLAGS),
        flops,
        12,
    )
    features_grad, got_x = together(features_grad, got_x)
    joined = call(
        join_kernel, shape((3, 16, 192), BF), (to_y, got_x), (VM, VM),
        [pltpu.VMEM((16, 192), F32)], 0, 2,
    )
    got_y = step(joined, "gy", 1)
    arrived, joined = together(arrived, joined)
    first, rest = split_sum(first, arrived, 4)
    part = sum_of((first, *turns(rest, 2, 8)))
    part = sum_of((part, *(swap(part, "gy", 8, d) for d in (1, 2, 3))))
    part, local = together(part, local)
    other = swap(part, "gy", 8, 4)
    output = call(
        output_kernel,
        shape((1, 1, 3, 64, 192), BF),
        (valid, local, got_x, got_y),
        (HB,) + (VM,) * 3,
        [pltpu.VMEM((64, 192), F32)] + [pltpu.VMEM((64, 128), F32)] * 2 + scalars(FLAGS),
        0,
    )
    other, output = together(other, output)
    weight_share = call(
        share_kernel,
        shape((162, 192), F32),
        (part, other),
        (VM, VM),
        [pltpu.VMEM((168, 192), F32)],
        0,
        2,
    )
    features_grad = jnp.swapaxes(features_grad, 3, 4)
    return output, features_grad, weight_share


def solution(mesh):
    return jax.shard_map(
        shards,
        mesh=mesh,
        in_specs=(
            P("gx", "gy", None, None, None),
            P(),
            P("gx", "gy", None, None, None),
            P("gx", "gy", None),
            P("gx", "gy", None, None),
            P("gx", "gy", None),
            P("gx", "gy", None, None, None),
            P("gx", "gy", None, None),
        ),
        out_specs=(P("gx", "gy", None, None, None), P("gx", "gy", None, None, None), P("gx", None)),
        check_vma=False,
    )
```

profile of v0, /device:TPU:128, one launch (start us, length us, event | category | flops | bytes accessed | tf_op | source)
XLA Modules:
  0.0 73.3 jit_solution(17768522984248483942)
XLA Ops:
  0.6 1.1 %shard_map.103 = (bf16[3,64,192]{2,1,0:T(8,128)(2,1)S(1)}, bf16[3,16,192]{2,1,0:T(8,128)(2,1)S(1)}) custom-call(s32[1,1,3]{2,1,0:T(1,128)} %valid_in.7, bf16[1,1,3,64,192]{4,3,2,1,0:T(8,128)(2,1)} %cot_in.1), custom_call_target="tpu_custom_call" | custom-call | bytes 73740 | tf_op jit(solution)/shard_map/pallas_call | solution.py:39
  1.8 1.3 %collective-permute-start = (bf16[3,16,192]{2,1,0:T(8,128)(2,1)S(1)}, bf16[3,16,192]{2,1,0:T(8,128)(2,1)S(1)}, u32[]{:S(2)}, u32[]{:S(2)}) collective-permute-start(bf16[3,16,192]{2,1,0:T(8,128)(2,1)S(1)} %get-tuple-element.42), channel_id=1, source_target_pairs={{8,0},{16,8},{24,16},{32,24},{40,32},{48,40},{56,48},{64,56},{72,6... | collective-permute-start | bytes 55304 | tf_op jit(solution)/shard_map/ppermute | solution.py:350
  3.1 1.8 %collective-permute-done.cot_x = bf16[3,16,192]{2,1,0:T(8,128)(2,1)S(1)} collective-permute-done((bf16[3,16,192]{2,1,0:T(8,128)(2,1)S(1)}, bf16[3,16,192]{2,1,0:T(8,128)(2,1)S(1)}, u32[]{:S(2)}, u32[]{:S(2)}) %collective-permute-start) | collective-permute-done | bytes 18464 | tf_op jit(solution)/shard_map/ppermute | solution.py:350
  4.9 2.8 %collective-permute-start.1 = (bf16[3,32,192]{2,1,0:T(8,128)(2,1)S(1)}, bf16[3,32,192]{2,1,0:T(8,128)(2,1)S(1)}, u32[]{:S(2)}, u32[]{:S(2)}) collective-permute-start(bf16[3,32,192]{2,1,0:T(8,128)(2,1)S(1)} %shard_map.104), channel_id=1, source_target_pairs={{1,0},{2,1},{3,2},{4,3},{5,4},{6,5},{7,6},{9,8},{10,9},{11,10},{12... | collective-permute-start | bytes 110600 | tf_op jit(solution)/shard_map/ppermute | solution.py:350
  7.7 1.7 %shard_map.105.split = bf16[8,192,192]{2,1,0:T(8,128)(2,1)S(1)} custom-call(s32[1,1,3]{2,1,0:T(1,128)} %valid_in.7, bf16[1,1,3,192,512]{4,3,2,1,0:T(8,128)(2,1)} %bitcast.7), custom_call_target="tpu_custom_call" | custom-call | bytes 589836 | tf_op jit(solution)/shard_map/pallas_call | solution.py:39
  9.5 1.4 %collective-permute-done.1.cot_y = bf16[3,32,192]{2,1,0:T(8,128)(2,1)S(1)} collective-permute-done((bf16[3,32,192]{2,1,0:T(8,128)(2,1)S(1)}, bf16[3,32,192]{2,1,0:T(8,128)(2,1)S(1)}, u32[]{:S(2)}, u32[]{:S(2)}) %collective-permute-start.1) | collective-permute-done | bytes 36896 | tf_op jit(solution)/shard_map/ppermute | solution.py:350
  10.9 2.6 %shard_map.106 = (f32[4096,128]{1,0:T(8,128)S(1)}, bf16[4096,128]{1,0:T(8,128)(2,1)S(1)}, bf16[8,192,192]{2,1,0:T(8,128)(2,1)S(1)}) custom-call(s32[1,1,2,12]{3,2,1,0:T(2,128)} %lrules_in.3, s32[1,1,12]{2,1,0:T(1,128)} %lcodes_in.3, s32[1,1,3,2,3]{4,3,2,1,0:T(2,128)} %bitcast.9, s32[1,3,1,3]{3,2,1,0:T(1,128)} %bitcast.11, ...), custom_call_target="tpu_custom_call" | custom-call | flops 382205952 | bytes 719100 | tf_op jit(solution)/shard_map/pallas_call | solution.py:39
  13.5 0.8 %collective-permute-start.2 = (bf16[4096,128]{1,0:T(8,128)(2,1)S(1)}, bf16[4096,128]{1,0:T(8,128)(2,1)S(1)}, u32[]{:S(2)}, u32[]{:S(2)}) collective-permute-start(bf16[4096,128]{1,0:T(8,128)(2,1)S(1)} %get-tuple-element.46), channel_id=1, source_target_pairs={{0,8},{8,0},{16,24},{24,16},{32,40},{40,32},{48,56},{56,48},{64,72... | collective-permute-start | bytes 3145736 | tf_op jit(solution)/shard_map/ppermute | solution.py:344
  14.3 2.1 %shard_map.107 = (f32[3,64,192]{2,1,0:T(8,128)S(1)}, bf16[3,32,192]{2,1,0:T(8,128)(2,1)S(1)}, f32[3,16,192]{2,1,0:T(8,128)S(1)}) custom-call(s32[1,1,2,12]{3,2,1,0:T(2,128)} %lrules_in.3, s32[1,1,12]{2,1,0:T(1,128)} %lcodes_in.3, s32[1,1,3,2,3]{4,3,2,1,0:T(2,128)} %bitcast.10, s32[1,3,1,3]{3,2,1,0:T(1,128)} %bitcast.12, ...), custom_call_target="tpu_custom_call" | custom-call | flops 382205952 | bytes 2580732 | tf_op jit(solution)/shard_map/pallas_call | solution.py:39
  16.4 0.2 collective-permute-done.2.refs_0_
  16.6 0.2 shard_map.108
  16.8 4.2 %collective-permute-start.3 = (bf16[1024,128]{1,0:T(8,128)(2,1)S(1)}, bf16[1024,128]{1,0:T(8,128)(2,1)S(1)}, u32[]{:S(2)}, u32[]{:S(2)}) collective-permute-start(bf16[1024,128]{1,0:T(8,128)(2,1)S(1)} %get-tuple-element.59), channel_id=1, source_target_pairs={{0,64},{8,24},{16,80},{24,8},{32,96},{40,56},{48,112},{56,40},{64,... | collective-permute-start | bytes 786440 | tf_op jit(solution)/shard_map/ppermute | solution.py:389
  21.0 3.2 %collective-permute-start.4 = (bf16[1024,128]{1,0:T(8,128)(2,1)S(1)}, bf16[1024,128]{1,0:T(8,128)(2,1)S(1)}, u32[]{:S(2)}, u32[]{:S(2)}) collective-permute-start(bf16[1024,128]{1,0:T(8,128)(2,1)S(1)} %get-tuple-element.60), channel_id=1, source_target_pairs={{0,128},{8,40},{16,144},{24,56},{32,160},{40,8},{48,176},{56,24},{... | collective-permute-start | bytes 786440 | tf_op jit(solution)/shard_map/ppermute | solution.py:389
  24.2 1.8 %collective-permute-start.6 = (bf16[3,32,192]{2,1,0:T(8,128)(2,1)S(1)}, bf16[3,32,192]{2,1,0:T(8,128)(2,1)S(1)}, u32[]{:S(2)}, u32[]{:S(2)}) collective-permute-start(bf16[3,32,192]{2,1,0:T(8,128)(2,1)S(1)} %get-tuple-element.64), channel_id=1, source_target_pairs={{0,8},{8,16},{16,24},{24,32},{32,40},{40,48},{48,56},{56,64},{64,7... | collective-permute-start | bytes 110600 | tf_op jit(solution)/shard_map/ppermute | solution.py:350
  26.0 3.4 %shard_map.109 = bf16[1,1,3,192,512]{4,3,2,1,0:T(8,128)(2,1)} custom-call(s32[1,1,3]{2,1,0:T(1,128)} %valid_in.7, bf16[8,192,192]{2,1,0:T(8,128)(2,1)S(1)} %get-tuple-element.63.shifts, bf16[192,5184]{1,0:T(8,128)(2,1)S(1)} %bitcast.6), custom_call_target="tpu_custom_call" | custom-call | flops 382205952 | bytes 2580492 | tf_op jit(solution)/shard_map/pallas_call | solution.py:39
  29.4 2.0 %collective-permute-done.4.refs_1_ = bf16[1024,128]{1,0:T(8,128)(2,1)S(1)} collective-permute-done((bf16[1024,128]{1,0:T(8,128)(2,1)S(1)}, bf16[1024,128]{1,0:T(8,128)(2,1)S(1)}, u32[]{:S(2)}, u32[]{:S(2)}) %collective-permute-start.4) | collective-permute-done | bytes 262176 | tf_op jit(solution)/shard_map/ppermute | solution.py:389
  31.4 2.7 %collective-permute-done.5.refs_2_ = bf16[1024,128]{1,0:T(8,128)(2,1)S(1)} collective-permute-done((bf16[1024,128]{1,0:T(8,128)(2,1)S(1)}, bf16[1024,128]{1,0:T(8,128)(2,1)S(1)}, u32[]{:S(2)}, u32[]{:S(2)}) %collective-permute-start.5) | collective-permute-done | bytes 262176 | tf_op jit(solution)/shard_map/ppermute | solution.py:389
  34.2 0.1 shard_map.111
  34.3 0.1 collective-permute-start.7
  34.4 4.6 %collective-permute-start.8 = (bf16[256,128]{1,0:T(8,128)(2,1)S(1)}, bf16[256,128]{1,0:T(8,128)(2,1)S(1)}, u32[]{:S(2)}, u32[]{:S(2)}) collective-permute-start(bf16[256,128]{1,0:T(8,128)(2,1)S(1)} %get-tuple-element.71), channel_id=1, source_target_pairs={{0,32},{8,136},{16,48},{24,152},{32,0},{40,168},{48,16},{56,184},{... | collective-permute-start | bytes 196616 | tf_op jit(solution)/shard_map/ppermute | solution.py:389
  39.0 1.4 %collective-permute-start.9 = (bf16[256,128]{1,0:T(8,128)(2,1)S(1)}, bf16[256,128]{1,0:T(8,128)(2,1)S(1)}, u32[]{:S(2)}, u32[]{:S(2)}) collective-permute-start(bf16[256,128]{1,0:T(8,128)(2,1)S(1)} %get-tuple-element.72), channel_id=1, source_target_pairs={{0,48},{8,200},{16,32},{24,216},{32,16},{40,232},{48,0},{56,248},{... | collective-permute-start | bytes 196616 | tf_op jit(solution)/shard_map/ppermute | solution.py:389
  40.4 0.9 %collective-permute-done.8.two = bf16[256,128]{1,0:T(8,128)(2,1)S(1)} collective-permute-done((bf16[256,128]{1,0:T(8,128)(2,1)S(1)}, bf16[256,128]{1,0:T(8,128)(2,1)S(1)}, u32[]{:S(2)}, u32[]{:S(2)}) %collective-permute-start.8) | collective-permute-done | bytes 65568 | tf_op jit(solution)/shard_map/ppermute | solution.py:389
  41.2 3.9 %collective-permute-done.9.three = bf16[256,128]{1,0:T(8,128)(2,1)S(1)} collective-permute-done((bf16[256,128]{1,0:T(8,128)(2,1)S(1)}, bf16[256,128]{1,0:T(8,128)(2,1)S(1)}, u32[]{:S(2)}, u32[]{:S(2)}) %collective-permute-start.9) | collective-permute-done | bytes 65568 | tf_op jit(solution)/shard_map/ppermute | solution.py:389
  45.3 1.3 %collective-permute-start.11 = (bf16[256,128]{1,0:T(8,128)(2,1)S(1)}, bf16[256,128]{1,0:T(8,128)(2,1)S(1)}, u32[]{:S(2)}, u32[]{:S(2)}) collective-permute-start(bf16[256,128]{1,0:T(8,128)(2,1)S(1)} %shard_map.112.first), channel_id=1, source_target_pairs={{0,2},{1,3},{2,0},{3,1},{4,6},{5,7},{6,4},{7,5},{8,10},{9,11},{10,... | collective-permute-start | bytes 196616 | tf_op jit(solution)/shard_map/ppermute | solution.py:344
  46.6 2.7 %collective-permute-start.10 = (bf16[256,128]{1,0:T(8,128)(2,1)S(1)}, bf16[256,128]{1,0:T(8,128)(2,1)S(1)}, u32[]{:S(2)}, u32[]{:S(2)}) collective-permute-start(bf16[256,128]{1,0:T(8,128)(2,1)S(1)} %shard_map.112.first), channel_id=1, source_target_pairs={{0,1},{1,0},{2,3},{3,2},{4,5},{5,4},{6,7},{7,6},{8,9},{9,8},{10,11... | collective-permute-start | bytes 196616 | tf_op jit(solution)/shard_map/ppermute | solution.py:344
  49.4 2.1 %collective-permute-done.12.three = bf16[256,128]{1,0:T(8,128)(2,1)S(1)} collective-permute-done((bf16[256,128]{1,0:T(8,128)(2,1)S(1)}, bf16[256,128]{1,0:T(8,128)(2,1)S(1)}, u32[]{:S(2)}, u32[]{:S(2)}) %collective-permute-start.12) | collective-permute-done | bytes 65568 | tf_op jit(solution)/shard_map/ppermute | solution.py:344
  51.5 0.9 %collective-permute-done.10.one = bf16[256,128]{1,0:T(8,128)(2,1)S(1)} collective-permute-done((bf16[256,128]{1,0:T(8,128)(2,1)S(1)}, bf16[256,128]{1,0:T(8,128)(2,1)S(1)}, u32[]{:S(2)}, u32[]{:S(2)}) %collective-permute-start.10) | collective-permute-done | bytes 65568 | tf_op jit(solution)/shard_map/ppermute | solution.py:344
  52.4 6.8 %collective-permute-start.13 = (bf16[256,128]{1,0:T(8,128)(2,1)S(1)}, bf16[256,128]{1,0:T(8,128)(2,1)S(1)}, u32[]{:S(2)}, u32[]{:S(2)}) collective-permute-start(bf16[256,128]{1,0:T(8,128)(2,1)S(1)} %shard_map.113.mine), channel_id=1, source_target_pairs={{0,4},{1,5},{2,6},{3,7},{4,0},{5,1},{6,2},{7,3},{8,12},{9,13},{10,... | collective-permute-start | bytes 196616 | tf_op jit(solution)/shard_map/ppermute | solution.py:344
  59.2 1.9 %collective-permute-start.14 = (bf16[3,16,192]{2,1,0:T(8,128)(2,1)S(1)}, bf16[3,16,192]{2,1,0:T(8,128)(2,1)S(1)}, u32[]{:S(2)}, u32[]{:S(2)}) collective-permute-start(bf16[3,16,192]{2,1,0:T(8,128)(2,1)S(1)} %shard_map.110), channel_id=1, source_target_pairs={{0,1},{1,2},{2,3},{3,4},{4,5},{5,6},{6,7},{8,9},{9,10},{10,11},{11... | collective-permute-start | bytes 55304 | tf_op jit(solution)/shard_map/ppermute | solution.py:350
  61.1 9.8 %collective-permute-done.14.got_y = bf16[3,16,192]{2,1,0:T(8,128)(2,1)S(1)} collective-permute-done((bf16[3,16,192]{2,1,0:T(8,128)(2,1)S(1)}, bf16[3,16,192]{2,1,0:T(8,128)(2,1)S(1)}, u32[]{:S(2)}, u32[]{:S(2)}) %collective-permute-start.14) | collective-permute-done | bytes 18464 | tf_op jit(solution)/shard_map/ppermute | solution.py:350
  70.9 1.5 %shard_map.114 = bf16[1,1,3,64,192]{4,3,2,1,0:T(8,128)(2,1)} custom-call(s32[1,1,3]{2,1,0:T(1,128)} %valid_in.7, f32[3,64,192]{2,1,0:T(8,128)S(1)} %get-tuple-element.75.local, bf16[3,32,192]{2,1,0:T(8,128)(2,1)S(1)} %collective-permute-done.6.got_x, bf16[3,16,192]{2,1,0:T(8,128)(2,1)S(1)} %collective-permute-done.14.got_y), custom_call_target="tpu_custom_call" | custom-call | bytes 202764 | tf_op jit(solution)/shard_map/pallas_call | solution.py:39
  72.5 0.8 %shard_map.115 = f32[162,192]{1,0:T(8,128)} custom-call(bf16[256,128]{1,0:T(8,128)(2,1)S(1)} %shard_map.113.mine, bf16[256,128]{1,0:T(8,128)(2,1)S(1)} %collective-permute-done.13.other), custom_call_target="tpu_custom_call" | custom-call | bytes 131072 | tf_op jit(solution)/shard_map/pallas_call | solution.py:39
  (13 shorter events, 0.2 us)
Async XLA Ops:
  0.6 13.7 %copy-start = (bf16[5184,192]{0,1:T(8,128)(2,1)S(1)}, bf16[5184,192]{0,1:T(8,128)(2,1)}, u32[]{:S(2)}) copy-start(bf16[5184,192]{0,1:T(8,128)(2,1)} %param.9) | copy-start | bytes 5971972
  1.8 3.1 %collective-permute-start = (bf16[3,16,192]{2,1,0:T(8,128)(2,1)S(1)}, bf16[3,16,192]{2,1,0:T(8,128)(2,1)S(1)}, u32[]{:S(2)}, u32[]{:S(2)}) collective-permute-start(bf16[3,16,192]{2,1,0:T(8,128)(2,1)S(1)} %get-tuple-element.42), channel_id=1, source_target_pairs={{8,0},{16,8},{24,16},{32,24},{40,32},{48,40},{56,48},{64,56},{72,6... | collective-permute-start | bytes 55304 | tf_op jit(solution)/shard_map/ppermute | solution.py:350
  4.9 6.0 %collective-permute-start.1 = (bf16[3,32,192]{2,1,0:T(8,128)(2,1)S(1)}, bf16[3,32,192]{2,1,0:T(8,128)(2,1)S(1)}, u32[]{:S(2)}, u32[]{:S(2)}) collective-permute-start(bf16[3,32,192]{2,1,0:T(8,128)(2,1)S(1)} %shard_map.104), channel_id=1, source_target_pairs={{1,0},{2,1},{3,2},{4,3},{5,4},{6,5},{7,6},{9,8},{10,9},{11,10},{12... | collective-permute-start | bytes 110600 | tf_op jit(solution)/shard_map/ppermute | solution.py:350
  13.5 3.1 %collective-permute-start.2 = (bf16[4096,128]{1,0:T(8,128)(2,1)S(1)}, bf16[4096,128]{1,0:T(8,128)(2,1)S(1)}, u32[]{:S(2)}, u32[]{:S(2)}) collective-permute-start(bf16[4096,128]{1,0:T(8,128)(2,1)S(1)} %get-tuple-element.46), channel_id=1, source_target_pairs={{0,8},{8,0},{16,24},{24,16},{32,40},{40,32},{48,56},{56,48},{64,72... | collective-permute-start | bytes 3145736 | tf_op jit(solution)/shard_map/ppermute | solution.py:344
  16.8 12.6 %collective-permute-start.3 = (bf16[1024,128]{1,0:T(8,128)(2,1)S(1)}, bf16[1024,128]{1,0:T(8,128)(2,1)S(1)}, u32[]{:S(2)}, u32[]{:S(2)}) collective-permute-start(bf16[1024,128]{1,0:T(8,128)(2,1)S(1)} %get-tuple-element.59), channel_id=1, source_target_pairs={{0,64},{8,24},{16,80},{24,8},{32,96},{40,56},{48,112},{56,40},{64,... | collective-permute-start | bytes 786440 | tf_op jit(solution)/shard_map/ppermute | solution.py:389
  21.0 10.4 %collective-permute-start.4 = (bf16[1024,128]{1,0:T(8,128)(2,1)S(1)}, bf16[1024,128]{1,0:T(8,128)(2,1)S(1)}, u32[]{:S(2)}, u32[]{:S(2)}) collective-permute-start(bf16[1024,128]{1,0:T(8,128)(2,1)S(1)} %get-tuple-element.60), channel_id=1, source_target_pairs={{0,128},{8,40},{16,144},{24,56},{32,160},{40,8},{48,176},{56,24},{... | collective-permute-start | bytes 786440 | tf_op jit(solution)/shard_map/ppermute | solution.py:389
  24.2 10.0 %collective-permute-start.5 = (bf16[1024,128]{1,0:T(8,128)(2,1)S(1)}, bf16[1024,128]{1,0:T(8,128)(2,1)S(1)}, u32[]{:S(2)}, u32[]{:S(2)}) collective-permute-start(bf16[1024,128]{1,0:T(8,128)(2,1)S(1)} %get-tuple-element.61), channel_id=1, source_target_pairs={{0,192},{8,56},{16,208},{24,40},{32,224},{40,24},{48,240},{56,8},{... | collective-permute-start | bytes 786440 | tf_op jit(solution)/shard_map/ppermute | solution.py:389
  24.2 5.2 %collective-permute-start.6 = (bf16[3,32,192]{2,1,0:T(8,128)(2,1)S(1)}, bf16[3,32,192]{2,1,0:T(8,128)(2,1)S(1)}, u32[]{:S(2)}, u32[]{:S(2)}) collective-permute-start(bf16[3,32,192]{2,1,0:T(8,128)(2,1)S(1)} %get-tuple-element.64), channel_id=1, source_target_pairs={{0,8},{8,16},{16,24},{24,32},{32,40},{40,48},{48,56},{56,64},{64,7... | collective-permute-start | bytes 110600 | tf_op jit(solution)/shard_map/ppermute | solution.py:350
  34.3 6.1 %collective-permute-start.7 = (bf16[256,128]{1,0:T(8,128)(2,1)S(1)}, bf16[256,128]{1,0:T(8,128)(2,1)S(1)}, u32[]{:S(2)}, u32[]{:S(2)}) collective-permute-start(bf16[256,128]{1,0:T(8,128)(2,1)S(1)} %get-tuple-element.70), channel_id=1, source_target_pairs={{0,16},{8,72},{16,0},{24,88},{32,48},{40,104},{48,32},{56,120},{64... | collective-permute-start | bytes 196616 | tf_op jit(solution)/shard_map/ppermute | solution.py:389
  34.4 6.9 %collective-permute-start.8 = (bf16[256,128]{1,0:T(8,128)(2,1)S(1)}, bf16[256,128]{1,0:T(8,128)(2,1)S(1)}, u32[]{:S(2)}, u32[]{:S(2)}) collective-permute-start(bf16[256,128]{1,0:T(8,128)(2,1)S(1)} %get-tuple-element.71), channel_id=1, source_target_pairs={{0,32},{8,136},{16,48},{24,152},{32,0},{40,168},{48,16},{56,184},{... | collective-permute-start | bytes 196616 | tf_op jit(solution)/shard_map/ppermute | solution.py:389
  39.0 6.2 %collective-permute-start.9 = (bf16[256,128]{1,0:T(8,128)(2,1)S(1)}, bf16[256,128]{1,0:T(8,128)(2,1)S(1)}, u32[]{:S(2)}, u32[]{:S(2)}) collective-permute-start(bf16[256,128]{1,0:T(8,128)(2,1)S(1)} %get-tuple-element.72), channel_id=1, source_target_pairs={{0,48},{8,200},{16,32},{24,216},{32,16},{40,232},{48,0},{56,248},{... | collective-permute-start | bytes 196616 | tf_op jit(solution)/shard_map/ppermute | solution.py:389
  45.2 6.3 %collective-permute-start.12 = (bf16[256,128]{1,0:T(8,128)(2,1)S(1)}, bf16[256,128]{1,0:T(8,128)(2,1)S(1)}, u32[]{:S(2)}, u32[]{:S(2)}) collective-permute-start(bf16[256,128]{1,0:T(8,128)(2,1)S(1)} %shard_map.112.first), channel_id=1, source_target_pairs={{0,3},{1,2},{2,1},{3,0},{4,7},{5,6},{6,5},{7,4},{8,11},{9,10},{10,... | collective-permute-start | bytes 196616 | tf_op jit(solution)/shard_map/ppermute | solution.py:344
  45.3 6.2 %collective-permute-start.11 = (bf16[256,128]{1,0:T(8,128)(2,1)S(1)}, bf16[256,128]{1,0:T(8,128)(2,1)S(1)}, u32[]{:S(2)}, u32[]{:S(2)}) collective-permute-start(bf16[256,128]{1,0:T(8,128)(2,1)S(1)} %shard_map.112.first), channel_id=1, source_target_pairs={{0,2},{1,3},{2,0},{3,1},{4,6},{5,7},{6,4},{7,5},{8,10},{9,11},{10,... | collective-permute-start | bytes 196616 | tf_op jit(solution)/shard_map/ppermute | solution.py:344
  46.6 5.7 %collective-permute-start.10 = (bf16[256,128]{1,0:T(8,128)(2,1)S(1)}, bf16[256,128]{1,0:T(8,128)(2,1)S(1)}, u32[]{:S(2)}, u32[]{:S(2)}) collective-permute-start(bf16[256,128]{1,0:T(8,128)(2,1)S(1)} %shard_map.112.first), channel_id=1, source_target_pairs={{0,1},{1,0},{2,3},{3,2},{4,5},{5,4},{6,7},{7,6},{8,9},{9,8},{10,11... | collective-permute-start | bytes 196616 | tf_op jit(solution)/shard_map/ppermute | solution.py:344
  52.4 20.1 %collective-permute-start.13 = (bf16[256,128]{1,0:T(8,128)(2,1)S(1)}, bf16[256,128]{1,0:T(8,128)(2,1)S(1)}, u32[]{:S(2)}, u32[]{:S(2)}) collective-permute-start(bf16[256,128]{1,0:T(8,128)(2,1)S(1)} %shard_map.113.mine), channel_id=1, source_target_pairs={{0,4},{1,5},{2,6},{3,7},{4,0},{5,1},{6,2},{7,3},{8,12},{9,13},{10,... | collective-permute-start | bytes 196616 | tf_op jit(solution)/shard_map/ppermute | solution.py:344
  59.2 11.7 %collective-permute-start.14 = (bf16[3,16,192]{2,1,0:T(8,128)(2,1)S(1)}, bf16[3,16,192]{2,1,0:T(8,128)(2,1)S(1)}, u32[]{:S(2)}, u32[]{:S(2)}) collective-permute-start(bf16[3,16,192]{2,1,0:T(8,128)(2,1)S(1)} %shard_map.110), channel_id=1, source_target_pairs={{0,1},{1,2},{2,3},{3,4},{4,5},{5,6},{6,7},{8,9},{9,10},{10,11},{11... | collective-permute-start | bytes 55304 | tf_op jit(solution)/shard_map/ppermute | solution.py:350
where the time goes:
time: 73.6 us; the launch traced here: 73.3 us
  starting transfers between devices  33.2 us (45%)
  waiting for transfers between devices  25.7 us (35%)
  Pallas kernels  13.7 us (19%)
  between operations  0.78 us (1%)
    pallas_call x13, Pallas kernels, call(): pl.pallas_call(kernel, out_shape=outs, in_specs=[pl.BlockSpec(memory_spac...  13.7 us
    ppermute x6, starting transfers between devices, turns(): got[d] = lax.ppermute(parts[d - 1], 'gx', route)  13.5 us
    ppermute x4, waiting for transfers between devices, step(): return lax.ppermute(value, axis, route)  13 us
    ppermute x5, starting transfers between devices, swap(): return lax.ppermute(value, axis, [(i, i ^ bits) for i in range(size)])  11.8 us
    ppermute x6, waiting for transfers between devices, turns(): got[d] = lax.ppermute(parts[d - 1], 'gx', route)  9.55 us
    ppermute x4, starting transfers between devices, step(): return lax.ppermute(value, axis, route)  7.83 us
    ppermute x5, waiting for transfers between devices, swap(): return lax.ppermute(value, axis, [(i, i ^ bits) for i in range(size)])  3.13 us
  transfers between devices with their start and end apart: 15, of which 10 were waited for; matrix products, arithmetic and copies ran while one was open for 0% of the time, Pallas kernels for 12%

commit v1 on v0

--- a/solution.py
+++ b/solution.py
@@ -86,22 +86,17 @@
             out[par, slot * 64 : slot * 64 + 64, :] = rows[par * 64 : par * 64 + 64]
 
 
-def mask_kernel(valid_in, cot_in, masked, face, cot, valid, sems):
+def mask_kernel(valid_in, cot_in, masked, face_x, face_y, edge, cot, valid, sems):
     for copy in fetch((valid_in, cot_in), (valid, cot), sems):
         copy.wait()
     for slot in range(3):
         rows = cot[0, 0, slot].astype(F32) * valid[0, 0, slot].astype(F32)
-        rows = rows.astype(BF)
-        masked[slot] = rows
-        face[slot] = rows[0:16]
-
-
-def pack_kernel(masked, cot_x, out):
-    for slot in range(3):
-        rows = masked[slot].astype(F32)
-        edge = cot_x[slot].astype(F32)[0:4]
-        face = [rows[p * 16 : p * 16 + 4] for p in range(4)]
-        out[slot] = jnp.concatenate(face + [edge, jnp.zeros((12, 192), F32)], axis=0).astype(BF)
+        masked[slot] = rows.astype(BF)
+        face_x[slot] = rows[0:16].astype(BF)
+        face_y[slot] = jnp.concatenate(
+            [rows[p * 16 : p * 16 + 4] for p in range(4)], axis=0
+        ).astype(BF)
+        edge[slot] = rows[0:8].astype(BF)
 
 
 def row_ids():
@@ -129,7 +124,7 @@
 
 
 def weight_kernel(
-    lrules_in, lcodes_in, rrules_in, rcodes_in, split, masked, cot_x, cot_y,
+    lrules_in, lcodes_in, rrules_in, rcodes_in, split, masked, cot_x, cot_y, cot_xy,
     keep, send, shifts, cubes, grads, low, high, total, lrules, lcodes, rrules, rcodes, sems,
 ):
     copies = fetch(
@@ -142,6 +137,7 @@
         cubes[slot] = to_cube_order(masked[slot].astype(F32), low, high)
         from_x = cot_x[slot].astype(F32)
         from_y = cot_y[slot].astype(F32)
+        from_xy = cot_xy[slot].astype(F32)
         for r in range(4):
             for n in range(4):
                 put = slice(r * 16 + n, r * 16 + n + 1)
@@ -149,7 +145,7 @@
                 put = slice(r * 16 + n * 4, r * 16 + n * 4 + 1)
                 cubes[8 + slot, put, :] = from_y[n * 4 + r : n * 4 + r + 1]
             put = slice(r * 16, r * 16 + 1)
-            cubes[12 + slot, put, :] = from_y[16 + r : 17 + r]
+            cubes[12 + slot, put, :] = from_xy[r : r + 1]
     for entry in range(32):
         grads[entry] = zero
     for copy in copies:
@@ -407,22 +403,28 @@
     features = jnp.swapaxes(features, 3, 4)
     shape = jax.ShapeDtypeStruct
     flops = 2 * 27 * 192**3
-    masked, face = call(
+    masked, face_x, face_y, edge = call(
         mask_kernel,
-        (shape((3, 64, 192), BF), shape((3, 16, 192), BF)),
+        (shape((3, 64, 192), BF),) + (shape((3, 16, 192), BF),) * 2 + (shape((3, 8, 192), BF),),
         (valid, cotangent),
         (HB, HB),
         [pltpu.VMEM((1, 1, 3, 64, 192), BF)] + scalars(FLAGS),
         0,
         2,
     )
-    cot_x = step(face, "gx", -1)
-    packed = call(pack_kernel, shape((3, 32, 192), BF), (masked, cot_x), (VM, VM), [], 0, 2)
-    cot_y = step(packed, "gy", -1)
+    cot_y = step(face_y, "gy", -1)
+    columns = lax.axis_size("gy")
+    route = [
+        (i * columns + j, (i - 1) * columns + j - 1)
+        for i in range(1, lax.axis_size("gx"))
+        for j in range(1, columns)
+    ]
+    cot_xy = lax.ppermute(edge, ("gx", "gy"), route)
+    cot_x = step(face_x, "gx", -1)
     split = call(
         split_kernel,
         shape((8, 192, 192), BF),
-        (valid, together(features, packed)[0]),
+        (valid, together(features, edge)[0]),
         (HB, HB),
         [pltpu.VMEM((1, 1, 3, 192, 512), BF)] + scalars(FLAGS),
         0,
@@ -431,8 +433,8 @@
     keep, send, shifts = call(
         weight_kernel,
         (shape((4096, 128), F32), shape((4096, 128), BF), shape((8, 192, 192), BF)),
-        (*rules, split, masked, cot_x, cot_y),
-        (HB,) * 4 + (VM,) * 4,
+        (*rules, split, masked, cot_x, cot_y, cot_xy),
+        (HB,) * 4 + (VM,) * 5,
         [pltpu.VMEM((16, 64, 192), F32), pltpu.VMEM((32, 64, 192), F32)]
         + [pltpu.VMEM((64, 128), F32)] * 2
         + [pltpu.VMEM((5184, 192), F32)]
@@ -466,16 +468,17 @@
         flops,
         12,
     )
-    features_grad, got_x = together(features_grad, got_x)
+    arrived, features_grad = together(arrived, features_grad)
+    first, rest = split_sum(first, arrived, 4)
+    part = sum_of((first, *turns(rest, 2, 8)))
+    part, to_y = together(part, to_y)
+    got = [swap(part, "gy", 8, d) for d in (1, 2, 3)]
     joined = call(
         join_kernel, shape((3, 16, 192), BF), (to_y, got_x), (VM, VM),
         [pltpu.VMEM((16, 192), F32)], 0, 2,
     )
     got_y = step(joined, "gy", 1)
-    arrived, joined = together(arrived, joined)
-    first, rest = split_sum(first, arrived, 4)
-    part = sum_of((first, *turns(rest, 2, 8)))
-    part = sum_of((part, *(swap(part, "gy", 8, d) for d in (1, 2, 3))))
+    part = sum_of((part, *got))
     part, local = together(part, local)
     other = swap(part, "gy", 8, 4)
     output = call(

time: 73.6 us -> 77.9 us (1.058)
  the two profiles are of different devices: /device:TPU:128 before, /device:TPU:224 now
where the time goes in v1:
time: 77.9 us; the launch traced here: 77.5 us
  starting transfers between devices  36.8 us (47%)
  waiting for transfers between devices  26.4 us (34%)
  Pallas kernels  13.6 us (17%)
  between operations  0.78 us (1%)
    ppermute x5, starting transfers between devices, swap(): return lax.ppermute(value, axis, [(i, i ^ bits) for i in range(size)])  14.3 us
    pallas_call x12, Pallas kernels, call(): pl.pallas_call(kernel, out_shape=outs, in_specs=[pl.BlockSpec(memory_spac...  13.6 us
    ppermute x4, waiting for transfers between devices, step(): return lax.ppermute(value, axis, route)  13.3 us
    ppermute x4, starting transfers between devices, step(): return lax.ppermute(value, axis, route)  11.3 us
    ppermute x6, starting transfers between devices, turns(): got[d] = lax.ppermute(parts[d - 1], 'gx', route)  9.25 us
    ppermute x6, waiting for transfers between devices, turns(): got[d] = lax.ppermute(parts[d - 1], 'gx', route)  8.6 us
    ppermute x5, waiting for transfers between devices, swap(): return lax.ppermute(value, axis, [(i, i ^ bits) for i in range(size)])  3.15 us
    ppermute x1, starting transfers between devices, shards(): cot_xy = lax.ppermute(edge, ('gx', 'gy'), route)  1.92 us
  transfers between devices with their start and end apart: 16, of which 10 were waited for; matrix products, arithmetic and copies ran while one was open for 0% of the time, Pallas kernels for 11%

profile of v1, /device:TPU:224, one launch (start us, length us, event | category | flops | bytes accessed | tf_op | source)
XLA Modules:
  0.0 77.5 jit_solution(17403703929732190845)
XLA Ops:
  0.6 1.1 %shard_map.103 = (bf16[3,64,192]{2,1,0:T(8,128)(2,1)S(1)}, bf16[3,16,192]{2,1,0:T(8,128)(2,1)S(1)}, bf16[3,16,192]{2,1,0:T(8,128)(2,1)S(1)}, bf16[3,8,192]{2,1,0:T(8,128)(2,1)S(1)}) custom-call(s32[1,1,3]{2,1,0:T(1,128)} %valid_in.7, bf16[1,1,3,64,192]{4,3,2,1,0:T(8,128)(2,1)} %cot_in.1), custom_call_target="tpu_custom_call" | custom-call | bytes 73740 | tf_op jit(solution)/shard_map/pallas_call | solution.py:39
  1.8 2.4 %collective-permute-start = (bf16[3,16,192]{2,1,0:T(8,128)(2,1)S(1)}, bf16[3,16,192]{2,1,0:T(8,128)(2,1)S(1)}, u32[]{:S(2)}, u32[]{:S(2)}) collective-permute-start(bf16[3,16,192]{2,1,0:T(8,128)(2,1)S(1)} %get-tuple-element.47), channel_id=1, source_target_pairs={{8,0},{16,8},{24,16},{32,24},{40,32},{48,40},{56,48},{64,56},{72,6... | collective-permute-start | bytes 55304 | tf_op jit(solution)/shard_map/ppermute | solution.py:346
  4.1 5.1 %collective-permute-start.1 = (bf16[3,16,192]{2,1,0:T(8,128)(2,1)S(1)}, bf16[3,16,192]{2,1,0:T(8,128)(2,1)S(1)}, u32[]{:S(2)}, u32[]{:S(2)}) collective-permute-start(bf16[3,16,192]{2,1,0:T(8,128)(2,1)S(1)} %get-tuple-element.48), channel_id=1, source_target_pairs={{1,0},{2,1},{3,2},{4,3},{5,4},{6,5},{7,6},{9,8},{10,9},{11,10},{12... | collective-permute-start | bytes 55304 | tf_op jit(solution)/shard_map/ppermute | solution.py:346
  9.3 1.9 %collective-permute-start.2 = (bf16[3,8,192]{2,1,0:T(8,128)(2,1)S(1)}, bf16[3,8,192]{2,1,0:T(8,128)(2,1)S(1)}, u32[]{:S(2)}, u32[]{:S(2)}) collective-permute-start(bf16[3,8,192]{2,1,0:T(8,128)(2,1)S(1)} %get-tuple-element.44), channel_id=1, source_target_pairs={{9,0},{10,1},{11,2},{12,3},{13,4},{14,5},{15,6},{17,8},{18,9},{19,... | collective-permute-start | bytes 27656 | tf_op jit(solution)/shard_map/ppermute | solution.py:422
  11.2 1.7 %shard_map.104.split = bf16[8,192,192]{2,1,0:T(8,128)(2,1)S(1)} custom-call(s32[1,1,3]{2,1,0:T(1,128)} %valid_in.7, bf16[1,1,3,192,512]{4,3,2,1,0:T(8,128)(2,1)} %bitcast.7), custom_call_target="tpu_custom_call" | custom-call | bytes 589836 | tf_op jit(solution)/shard_map/pallas_call | solution.py:39
  12.9 1.3 %collective-permute-done.2.cot_xy = bf16[3,8,192]{2,1,0:T(8,128)(2,1)S(1)} collective-permute-done((bf16[3,8,192]{2,1,0:T(8,128)(2,1)S(1)}, bf16[3,8,192]{2,1,0:T(8,128)(2,1)S(1)}, u32[]{:S(2)}, u32[]{:S(2)}) %collective-permute-start.2) | collective-permute-done | bytes 9248 | tf_op jit(solution)/shard_map/ppermute | solution.py:422
  14.3 2.6 %shard_map.105 = (f32[4096,128]{1,0:T(8,128)S(1)}, bf16[4096,128]{1,0:T(8,128)(2,1)S(1)}, bf16[8,192,192]{2,1,0:T(8,128)(2,1)S(1)}) custom-call(s32[1,1,2,12]{3,2,1,0:T(2,128)} %lrules_in.3, s32[1,1,12]{2,1,0:T(1,128)} %lcodes_in.3, s32[1,1,3,2,3]{4,3,2,1,0:T(2,128)} %bitcast.9, s32[1,3,1,3]{3,2,1,0:T(1,128)} %bitcast.11, ...), custom_call_target="tpu_custom_call" | custom-call | flops 382205952 | bytes 709884 | tf_op jit(solution)/shard_map/pallas_call | solution.py:39
  16.9 3.9 %collective-permute-start.3 = (bf16[4096,128]{1,0:T(8,128)(2,1)S(1)}, bf16[4096,128]{1,0:T(8,128)(2,1)S(1)}, u32[]{:S(2)}, u32[]{:S(2)}) collective-permute-start(bf16[4096,128]{1,0:T(8,128)(2,1)S(1)} %get-tuple-element.51), channel_id=1, source_target_pairs={{0,8},{8,0},{16,24},{24,16},{32,40},{40,32},{48,56},{56,48},{64,72... | collective-permute-start | bytes 3145736 | tf_op jit(solution)/shard_map/ppermute | solution.py:340
  20.8 2.1 %shard_map.106 = (f32[3,64,192]{2,1,0:T(8,128)S(1)}, bf16[3,32,192]{2,1,0:T(8,128)(2,1)S(1)}, f32[3,16,192]{2,1,0:T(8,128)S(1)}) custom-call(s32[1,1,2,12]{3,2,1,0:T(2,128)} %lrules_in.3, s32[1,1,12]{2,1,0:T(1,128)} %lcodes_in.3, s32[1,1,3,2,3]{4,3,2,1,0:T(2,128)} %bitcast.10, s32[1,3,1,3]{3,2,1,0:T(1,128)} %bitcast.12, ...), custom_call_target="tpu_custom_call" | custom-call | flops 382205952 | bytes 2580732 | tf_op jit(solution)/shard_map/pallas_call | solution.py:39
  22.9 0.2 collective-permute-done.3.refs_0_
  23.1 0.2 shard_map.107
  23.3 1.7 %collective-permute-start.4 = (bf16[1024,128]{1,0:T(8,128)(2,1)S(1)}, bf16[1024,128]{1,0:T(8,128)(2,1)S(1)}, u32[]{:S(2)}, u32[]{:S(2)}) collective-permute-start(bf16[1024,128]{1,0:T(8,128)(2,1)S(1)} %get-tuple-element.64), channel_id=1, source_target_pairs={{0,64},{8,24},{16,80},{24,8},{32,96},{40,56},{48,112},{56,40},{64,... | collective-permute-start | bytes 786440 | tf_op jit(solution)/shard_map/ppermute | solution.py:385
  24.9 1.7 %collective-permute-start.5 = (bf16[1024,128]{1,0:T(8,128)(2,1)S(1)}, bf16[1024,128]{1,0:T(8,128)(2,1)S(1)}, u32[]{:S(2)}, u32[]{:S(2)}) collective-permute-start(bf16[1024,128]{1,0:T(8,128)(2,1)S(1)} %get-tuple-element.65), channel_id=1, source_target_pairs={{0,128},{8,40},{16,144},{24,56},{32,160},{40,8},{48,176},{56,24},{... | collective-permute-start | bytes 786440 | tf_op jit(solution)/shard_map/ppermute | solution.py:385
  26.6 1.4 %collective-permute-start.6 = (bf16[1024,128]{1,0:T(8,128)(2,1)S(1)}, bf16[1024,128]{1,0:T(8,128)(2,1)S(1)}, u32[]{:S(2)}, u32[]{:S(2)}) collective-permute-start(bf16[1024,128]{1,0:T(8,128)(2,1)S(1)} %get-tuple-element.66), channel_id=1, source_target_pairs={{0,192},{8,56},{16,208},{24,40},{32,224},{40,24},{48,240},{56,8},{... | collective-permute-start | bytes 786440 | tf_op jit(solution)/shard_map/ppermute | solution.py:385
  28.0 3.4 %shard_map.108 = bf16[1,1,3,192,512]{4,3,2,1,0:T(8,128)(2,1)} custom-call(s32[1,1,3]{2,1,0:T(1,128)} %valid_in.7, bf16[8,192,192]{2,1,0:T(8,128)(2,1)S(1)} %get-tuple-element.67.shifts, bf16[192,5184]{1,0:T(8,128)(2,1)S(1)} %bitcast.6), custom_call_target="tpu_custom_call" | custom-call | flops 382205952 | bytes 2580492 | tf_op jit(solution)/shard_map/pallas_call | solution.py:39
  31.4 2.4 %collective-permute-done.5.refs_1_ = bf16[1024,128]{1,0:T(8,128)(2,1)S(1)} collective-permute-done((bf16[1024,128]{1,0:T(8,128)(2,1)S(1)}, bf16[1024,128]{1,0:T(8,128)(2,1)S(1)}, u32[]{:S(2)}, u32[]{:S(2)}) %collective-permute-start.5) | collective-permute-done | bytes 262176 | tf_op jit(solution)/shard_map/ppermute | solution.py:385
  33.8 2.7 %collective-permute-done.6.refs_2_ = bf16[1024,128]{1,0:T(8,128)(2,1)S(1)} collective-permute-done((bf16[1024,128]{1,0:T(8,128)(2,1)S(1)}, bf16[1024,128]{1,0:T(8,128)(2,1)S(1)}, u32[]{:S(2)}, u32[]{:S(2)}) %collective-permute-start.6) | collective-permute-done | bytes 262176 | tf_op jit(solution)/shard_map/ppermute | solution.py:385
  36.7 1.8 %collective-permute-start.8 = (bf16[256,128]{1,0:T(8,128)(2,1)S(1)}, bf16[256,128]{1,0:T(8,128)(2,1)S(1)}, u32[]{:S(2)}, u32[]{:S(2)}) collective-permute-start(bf16[256,128]{1,0:T(8,128)(2,1)S(1)} %get-tuple-element.73), channel_id=1, source_target_pairs={{0,32},{8,136},{16,48},{24,152},{32,0},{40,168},{48,16},{56,184},{... | collective-permute-start | bytes 196616 | tf_op jit(solution)/shard_map/ppermute | solution.py:385
  38.5 2.6 %collective-permute-start.9 = (bf16[256,128]{1,0:T(8,128)(2,1)S(1)}, bf16[256,128]{1,0:T(8,128)(2,1)S(1)}, u32[]{:S(2)}, u32[]{:S(2)}) collective-permute-start(bf16[256,128]{1,0:T(8,128)(2,1)S(1)} %get-tuple-element.74), channel_id=1, source_target_pairs={{0,48},{8,200},{16,32},{24,216},{32,16},{40,232},{48,0},{56,248},{... | collective-permute-start | bytes 196616 | tf_op jit(solution)/shard_map/ppermute | solution.py:385
  41.1 0.9 %collective-permute-done.8.two = bf16[256,128]{1,0:T(8,128)(2,1)S(1)} collective-permute-done((bf16[256,128]{1,0:T(8,128)(2,1)S(1)}, bf16[256,128]{1,0:T(8,128)(2,1)S(1)}, u32[]{:S(2)}, u32[]{:S(2)}) %collective-permute-start.8) | collective-permute-done | bytes 65568 | tf_op jit(solution)/shard_map/ppermute | solution.py:385
  42.0 2.6 %collective-permute-done.9.three = bf16[256,128]{1,0:T(8,128)(2,1)S(1)} collective-permute-done((bf16[256,128]{1,0:T(8,128)(2,1)S(1)}, bf16[256,128]{1,0:T(8,128)(2,1)S(1)}, u32[]{:S(2)}, u32[]{:S(2)}) %collective-permute-start.9) | collective-permute-done | bytes 65568 | tf_op jit(solution)/shard_map/ppermute | solution.py:385
  44.7 2.6 %collective-permute-start.11 = (bf16[256,128]{1,0:T(8,128)(2,1)S(1)}, bf16[256,128]{1,0:T(8,128)(2,1)S(1)}, u32[]{:S(2)}, u32[]{:S(2)}) collective-permute-start(bf16[256,128]{1,0:T(8,128)(2,1)S(1)} %shard_map.110.first), channel_id=1, source_target_pairs={{0,2},{1,3},{2,0},{3,1},{4,6},{5,7},{6,4},{7,5},{8,10},{9,11},{10,... | collective-permute-start | bytes 196616 | tf_op jit(solution)/shard_map/ppermute | solution.py:340
  47.3 1.5 %collective-permute-start.10 = (bf16[256,128]{1,0:T(8,128)(2,1)S(1)}, bf16[256,128]{1,0:T(8,128)(2,1)S(1)}, u32[]{:S(2)}, u32[]{:S(2)}) collective-permute-start(bf16[256,128]{1,0:T(8,128)(2,1)S(1)} %shard_map.110.first), channel_id=1, source_target_pairs={{0,1},{1,0},{2,3},{3,2},{4,5},{5,4},{6,7},{7,6},{8,9},{9,8},{10,11... | collective-permute-start | bytes 196616 | tf_op jit(solution)/shard_map/ppermute | solution.py:340
  48.8 2.1 %collective-permute-done.12.three = bf16[256,128]{1,0:T(8,128)(2,1)S(1)} collective-permute-done((bf16[256,128]{1,0:T(8,128)(2,1)S(1)}, bf16[256,128]{1,0:T(8,128)(2,1)S(1)}, u32[]{:S(2)}, u32[]{:S(2)}) %collective-permute-start.12) | collective-permute-done | bytes 65568 | tf_op jit(solution)/shard_map/ppermute | solution.py:340
  50.9 0.9 %collective-permute-done.10.one = bf16[256,128]{1,0:T(8,128)(2,1)S(1)} collective-permute-done((bf16[256,128]{1,0:T(8,128)(2,1)S(1)}, bf16[256,128]{1,0:T(8,128)(2,1)S(1)}, u32[]{:S(2)}, u32[]{:S(2)}) %collective-permute-start.10) | collective-permute-done | bytes 65568 | tf_op jit(solution)/shard_map/ppermute | solution.py:340
  51.8 6.2 %collective-permute-start.13 = (bf16[256,128]{1,0:T(8,128)(2,1)S(1)}, bf16[256,128]{1,0:T(8,128)(2,1)S(1)}, u32[]{:S(2)}, u32[]{:S(2)}) collective-permute-start(bf16[256,128]{1,0:T(8,128)(2,1)S(1)} %shard_map.111.mine), channel_id=1, source_target_pairs={{0,4},{1,5},{2,6},{3,7},{4,0},{5,1},{6,2},{7,3},{8,12},{9,13},{10,... | collective-permute-start | bytes 196616 | tf_op jit(solution)/shard_map/ppermute | solution.py:340
  58.0 1.9 %collective-permute-start.14 = (bf16[3,32,192]{2,1,0:T(8,128)(2,1)S(1)}, bf16[3,32,192]{2,1,0:T(8,128)(2,1)S(1)}, u32[]{:S(2)}, u32[]{:S(2)}) collective-permute-start(bf16[3,32,192]{2,1,0:T(8,128)(2,1)S(1)} %get-tuple-element.80), channel_id=1, source_target_pairs={{0,8},{8,16},{16,24},{24,32},{32,40},{40,48},{48,56},{56,64},{64,7... | collective-permute-start | bytes 110600 | tf_op jit(solution)/shard_map/ppermute | solution.py:346
  60.0 3.5 %collective-permute-done.14.got_x = bf16[3,32,192]{2,1,0:T(8,128)(2,1)S(1)} collective-permute-done((bf16[3,32,192]{2,1,0:T(8,128)(2,1)S(1)}, bf16[3,32,192]{2,1,0:T(8,128)(2,1)S(1)}, u32[]{:S(2)}, u32[]{:S(2)}) %collective-permute-start.14) | collective-permute-done | bytes 36896 | tf_op jit(solution)/shard_map/ppermute | solution.py:346
  63.5 1.9 %collective-permute-start.15 = (bf16[3,16,192]{2,1,0:T(8,128)(2,1)S(1)}, bf16[3,16,192]{2,1,0:T(8,128)(2,1)S(1)}, u32[]{:S(2)}, u32[]{:S(2)}) collective-permute-start(bf16[3,16,192]{2,1,0:T(8,128)(2,1)S(1)} %shard_map.112), channel_id=1, source_target_pairs={{0,1},{1,2},{2,3},{3,4},{4,5},{5,6},{6,7},{8,9},{9,10},{10,11},{11... | collective-permute-start | bytes 55304 | tf_op jit(solution)/shard_map/ppermute | solution.py:346
  65.4 9.8 %collective-permute-done.15.got_y = bf16[3,16,192]{2,1,0:T(8,128)(2,1)S(1)} collective-permute-done((bf16[3,16,192]{2,1,0:T(8,128)(2,1)S(1)}, bf16[3,16,192]{2,1,0:T(8,128)(2,1)S(1)}, u32[]{:S(2)}, u32[]{:S(2)}) %collective-permute-start.15) | collective-permute-done | bytes 18464 | tf_op jit(solution)/shard_map/ppermute | solution.py:346
  75.2 1.5 %shard_map.113 = bf16[1,1,3,64,192]{4,3,2,1,0:T(8,128)(2,1)} custom-call(s32[1,1,3]{2,1,0:T(1,128)} %valid_in.7, f32[3,64,192]{2,1,0:T(8,128)S(1)} %get-tuple-element.79.local, bf16[3,32,192]{2,1,0:T(8,128)(2,1)S(1)} %collective-permute-done.14.got_x, bf16[3,16,192]{2,1,0:T(8,128)(2,1)S(1)} %collective-permute-done.15.got_y), custom_call_target="tpu_custom_call" | custom-call | bytes 202764 | tf_op jit(solution)/shard_map/pallas_call | solution.py:39
  76.8 0.8 shard_map.114
  (14 shorter events, 0.4 us)
Async XLA Ops:
  0.6 20.2 %copy-start = (bf16[5184,192]{0,1:T(8,128)(2,1)S(1)}, bf16[5184,192]{0,1:T(8,128)(2,1)}, u32[]{:S(2)}) copy-start(bf16[5184,192]{0,1:T(8,128)(2,1)} %param.9) | copy-start | bytes 5971972
  1.8 12.5 %collective-permute-start = (bf16[3,16,192]{2,1,0:T(8,128)(2,1)S(1)}, bf16[3,16,192]{2,1,0:T(8,128)(2,1)S(1)}, u32[]{:S(2)}, u32[]{:S(2)}) collective-permute-start(bf16[3,16,192]{2,1,0:T(8,128)(2,1)S(1)} %get-tuple-element.47), channel_id=1, source_target_pairs={{8,0},{16,8},{24,16},{32,24},{40,32},{48,40},{56,48},{64,56},{72,6... | collective-permute-start | bytes 55304 | tf_op jit(solution)/shard_map/ppermute | solution.py:346
  4.1 10.1 %collective-permute-start.1 = (bf16[3,16,192]{2,1,0:T(8,128)(2,1)S(1)}, bf16[3,16,192]{2,1,0:T(8,128)(2,1)S(1)}, u32[]{:S(2)}, u32[]{:S(2)}) collective-permute-start(bf16[3,16,192]{2,1,0:T(8,128)(2,1)S(1)} %get-tuple-element.48), channel_id=1, source_target_pairs={{1,0},{2,1},{3,2},{4,3},{5,4},{6,5},{7,6},{9,8},{10,9},{11,10},{12... | collective-permute-start | bytes 55304 | tf_op jit(solution)/shard_map/ppermute | solution.py:346
  9.3 5.0 %collective-permute-start.2 = (bf16[3,8,192]{2,1,0:T(8,128)(2,1)S(1)}, bf16[3,8,192]{2,1,0:T(8,128)(2,1)S(1)}, u32[]{:S(2)}, u32[]{:S(2)}) collective-permute-start(bf16[3,8,192]{2,1,0:T(8,128)(2,1)S(1)} %get-tuple-element.44), channel_id=1, source_target_pairs={{9,0},{10,1},{11,2},{12,3},{13,4},{14,5},{15,6},{17,8},{18,9},{19,... | collective-permute-start | bytes 27656 | tf_op jit(solution)/shard_map/ppermute | solution.py:422
  16.9 6.2 %collective-permute-start.3 = (bf16[4096,128]{1,0:T(8,128)(2,1)S(1)}, bf16[4096,128]{1,0:T(8,128)(2,1)S(1)}, u32[]{:S(2)}, u32[]{:S(2)}) collective-permute-start(bf16[4096,128]{1,0:T(8,128)(2,1)S(1)} %get-tuple-element.51), channel_id=1, source_target_pairs={{0,8},{8,0},{16,24},{24,16},{32,40},{40,32},{48,56},{56,48},{64,72... | collective-permute-start | bytes 3145736 | tf_op jit(solution)/shard_map/ppermute | solution.py:340
  23.3 8.1 %collective-permute-start.4 = (bf16[1024,128]{1,0:T(8,128)(2,1)S(1)}, bf16[1024,128]{1,0:T(8,128)(2,1)S(1)}, u32[]{:S(2)}, u32[]{:S(2)}) collective-permute-start(bf16[1024,128]{1,0:T(8,128)(2,1)S(1)} %get-tuple-element.64), channel_id=1, source_target_pairs={{0,64},{8,24},{16,80},{24,8},{32,96},{40,56},{48,112},{56,40},{64,... | collective-permute-start | bytes 786440 | tf_op jit(solution)/shard_map/ppermute | solution.py:385
  24.9 8.9 %collective-permute-start.5 = (bf16[1024,128]{1,0:T(8,128)(2,1)S(1)}, bf16[1024,128]{1,0:T(8,128)(2,1)S(1)}, u32[]{:S(2)}, u32[]{:S(2)}) collective-permute-start(bf16[1024,128]{1,0:T(8,128)(2,1)S(1)} %get-tuple-element.65), channel_id=1, source_target_pairs={{0,128},{8,40},{16,144},{24,56},{32,160},{40,8},{48,176},{56,24},{... | collective-permute-start | bytes 786440 | tf_op jit(solution)/shard_map/ppermute | solution.py:385
  26.6 9.9 %collective-permute-start.6 = (bf16[1024,128]{1,0:T(8,128)(2,1)S(1)}, bf16[1024,128]{1,0:T(8,128)(2,1)S(1)}, u32[]{:S(2)}, u32[]{:S(2)}) collective-permute-start(bf16[1024,128]{1,0:T(8,128)(2,1)S(1)} %get-tuple-element.66), channel_id=1, source_target_pairs={{0,192},{8,56},{16,208},{24,40},{32,224},{40,24},{48,240},{56,8},{... | collective-permute-start | bytes 786440 | tf_op jit(solution)/shard_map/ppermute | solution.py:385
  36.6 4.5 %collective-permute-start.7 = (bf16[256,128]{1,0:T(8,128)(2,1)S(1)}, bf16[256,128]{1,0:T(8,128)(2,1)S(1)}, u32[]{:S(2)}, u32[]{:S(2)}) collective-permute-start(bf16[256,128]{1,0:T(8,128)(2,1)S(1)} %get-tuple-element.72), channel_id=1, source_target_pairs={{0,16},{8,72},{16,0},{24,88},{32,48},{40,104},{48,32},{56,120},{64... | collective-permute-start | bytes 196616 | tf_op jit(solution)/shard_map/ppermute | solution.py:385
  36.7 5.3 %collective-permute-start.8 = (bf16[256,128]{1,0:T(8,128)(2,1)S(1)}, bf16[256,128]{1,0:T(8,128)(2,1)S(1)}, u32[]{:S(2)}, u32[]{:S(2)}) collective-permute-start(bf16[256,128]{1,0:T(8,128)(2,1)S(1)} %get-tuple-element.73), channel_id=1, source_target_pairs={{0,32},{8,136},{16,48},{24,152},{32,0},{40,168},{48,16},{56,184},{... | collective-permute-start | bytes 196616 | tf_op jit(solution)/shard_map/ppermute | solution.py:385
  38.5 6.1 %collective-permute-start.9 = (bf16[256,128]{1,0:T(8,128)(2,1)S(1)}, bf16[256,128]{1,0:T(8,128)(2,1)S(1)}, u32[]{:S(2)}, u32[]{:S(2)}) collective-permute-start(bf16[256,128]{1,0:T(8,128)(2,1)S(1)} %get-tuple-element.74), channel_id=1, source_target_pairs={{0,48},{8,200},{16,32},{24,216},{32,16},{40,232},{48,0},{56,248},{... | collective-permute-start | bytes 196616 | tf_op jit(solution)/shard_map/ppermute | solution.py:385
  44.6 6.3 %collective-permute-start.12 = (bf16[256,128]{1,0:T(8,128)(2,1)S(1)}, bf16[256,128]{1,0:T(8,128)(2,1)S(1)}, u32[]{:S(2)}, u32[]{:S(2)}) collective-permute-start(bf16[256,128]{1,0:T(8,128)(2,1)S(1)} %shard_map.110.first), channel_id=1, source_target_pairs={{0,3},{1,2},{2,1},{3,0},{4,7},{5,6},{6,5},{7,4},{8,11},{9,10},{10,... | collective-permute-start | bytes 196616 | tf_op jit(solution)/shard_map/ppermute | solution.py:340
  44.7 6.2 %collective-permute-start.11 = (bf16[256,128]{1,0:T(8,128)(2,1)S(1)}, bf16[256,128]{1,0:T(8,128)(2,1)S(1)}, u32[]{:S(2)}, u32[]{:S(2)}) collective-permute-start(bf16[256,128]{1,0:T(8,128)(2,1)S(1)} %shard_map.110.first), channel_id=1, source_target_pairs={{0,2},{1,3},{2,0},{3,1},{4,6},{5,7},{6,4},{7,5},{8,10},{9,11},{10,... | collective-permute-start | bytes 196616 | tf_op jit(solution)/shard_map/ppermute | solution.py:340
  47.3 4.4 %collective-permute-start.10 = (bf16[256,128]{1,0:T(8,128)(2,1)S(1)}, bf16[256,128]{1,0:T(8,128)(2,1)S(1)}, u32[]{:S(2)}, u32[]{:S(2)}) collective-permute-start(bf16[256,128]{1,0:T(8,128)(2,1)S(1)} %shard_map.110.first), channel_id=1, source_target_pairs={{0,1},{1,0},{2,3},{3,2},{4,5},{5,4},{6,7},{7,6},{8,9},{9,8},{10,11... | collective-permute-start | bytes 196616 | tf_op jit(solution)/shard_map/ppermute | solution.py:340
  51.8 25.0 %collective-permute-start.13 = (bf16[256,128]{1,0:T(8,128)(2,1)S(1)}, bf16[256,128]{1,0:T(8,128)(2,1)S(1)}, u32[]{:S(2)}, u32[]{:S(2)}) collective-permute-start(bf16[256,128]{1,0:T(8,128)(2,1)S(1)} %shard_map.111.mine), channel_id=1, source_target_pairs={{0,4},{1,5},{2,6},{3,7},{4,0},{5,1},{6,2},{7,3},{8,12},{9,13},{10,... | collective-permute-start | bytes 196616 | tf_op jit(solution)/shard_map/ppermute | solution.py:340
  58.0 5.4 %collective-permute-start.14 = (bf16[3,32,192]{2,1,0:T(8,128)(2,1)S(1)}, bf16[3,32,192]{2,1,0:T(8,128)(2,1)S(1)}, u32[]{:S(2)}, u32[]{:S(2)}) collective-permute-start(bf16[3,32,192]{2,1,0:T(8,128)(2,1)S(1)} %get-tuple-element.80), channel_id=1, source_target_pairs={{0,8},{8,16},{16,24},{24,32},{32,40},{40,48},{48,56},{56,64},{64,7... | collective-permute-start | bytes 110600 | tf_op jit(solution)/shard_map/ppermute | solution.py:346
  63.5 11.7 %collective-permute-start.15 = (bf16[3,16,192]{2,1,0:T(8,128)(2,1)S(1)}, bf16[3,16,192]{2,1,0:T(8,128)(2,1)S(1)}, u32[]{:S(2)}, u32[]{:S(2)}) collective-permute-start(bf16[3,16,192]{2,1,0:T(8,128)(2,1)S(1)} %shard_map.112), channel_id=1, source_target_pairs={{0,1},{1,2},{2,3},{3,4},{4,5},{5,6},{6,7},{8,9},{9,10},{10,11},{11... | collective-permute-start | bytes 55304 | tf_op jit(solution)/shard_map/ppermute | solution.py:346

commit v2 on v1

--- a/solution.py
+++ b/solution.py
@@ -72,10 +72,10 @@
     return jnp.where(voxel == x * 64 + y * 8 + z, 1.0, 0.0).astype(BF)
 
 
-def split_kernel(valid_in, feat_in, out, feat, valid, sems):
-    copies = fetch((valid_in, feat_in), (valid, feat), sems)
+def split_kernel(valid_in, feat_in, weight_in, out, weight, feat, valid, sems):
+    copies = fetch((valid_in, feat_in, weight_in), (valid, feat, weight), sems)
     order = parity_order()
-    for copy in copies:
+    for copy in copies[:2]:
         copy.wait()
     for slot in range(3):
         rows = lax.dot_general(
@@ -84,6 +84,7 @@
         rows = (rows * valid[0, 0, slot].astype(F32)).astype(BF)
         for par in range(8):
             out[par, slot * 64 : slot * 64 + 64, :] = rows[par * 64 : par * 64 + 64]
+    copies[2].wait()
 
 
 def mask_kernel(valid_in, cot_in, masked, face_x, face_y, edge, cot, valid, sems):
@@ -421,15 +422,26 @@
     ]
     cot_xy = lax.ppermute(edge, ("gx", "gy"), route)
     cot_x = step(face_x, "gx", -1)
-    split = call(
+    split, weight = call(
         split_kernel,
-        shape((8, 192, 192), BF),
-        (valid, together(features, edge)[0]),
-        (HB, HB),
+        (shape((8, 192, 192), BF), shape((192, 5184), BF)),
+        (valid, together(features, edge)[0], weight),
+        (HB,) * 3,
         [pltpu.VMEM((1, 1, 3, 192, 512), BF)] + scalars(FLAGS),
-        0,
-        6,
-    )
+        flops,
+        10,
+    )
+    local, to_x, to_y = call(
+        forward_kernel,
+        (shape((3, 64, 192), F32), shape((3, 32, 192), BF), shape((3, 16, 192), F32)),
+        (*rules, split, weight),
+        (HB,) * 4 + (VM,) * 2,
+        [pltpu.VMEM((24, 64, 192), F32), pltpu.VMEM((16, 64, 192), F32), pltpu.VMEM((32, 192), F32)]
+        + scalars(TABLES),
+        flops,
+        12,
+    )
+    split, local, to_x, to_y = together(split, local, to_x, to_y)
     keep, send, shifts = call(
         weight_kernel,
         (shape((4096, 128), F32), shape((4096, 128), BF), shape((8, 192, 192), BF)),
@@ -442,23 +454,12 @@
         flops,
         18,
     )
-    send, split, weight = together(send, split, weight)
+    send, to_x = together(send, to_x)
     arrived = swap(send, "gx", 32, 1)
-    local, to_x, to_y = call(
-        forward_kernel,
-        (shape((3, 64, 192), F32), shape((3, 32, 192), BF), shape((3, 16, 192), F32)),
-        (*rules, split, weight),
-        (HB,) * 4 + (VM,) * 2,
-        [pltpu.VMEM((24, 64, 192), F32), pltpu.VMEM((16, 64, 192), F32), pltpu.VMEM((32, 192), F32)]
-        + scalars(TABLES),
-        flops,
-        12,
-    )
-    arrived, local, to_x, to_y = together(arrived, local, to_x, to_y)
+    got_x = step(to_x, "gx", 1)
     first, rest = split_sum(keep, [arrived], 8)
-    rest, shifts, to_x = together(rest, shifts, to_x)
+    rest, shifts = together(rest, shifts)
     arrived = turns(rest, 8, 2)
-    got_x = step(to_x, "gx", 1)
     features_grad = call(
         features_kernel,
         shape((1, 1, 3, 192, 512), BF),
@@ -468,16 +469,16 @@
         flops,
         12,
     )
+    features_grad, got_x, to_y = together(features_grad, got_x, to_y)
+    joined = call(
+        join_kernel, shape((3, 16, 192), BF), (to_y, got_x), (VM, VM),
+        [pltpu.VMEM((16, 192), F32)], 0, 2,
+    )
+    got_y = step(joined, "gy", 1)
     arrived, features_grad = together(arrived, features_grad)
     first, rest = split_sum(first, arrived, 4)
     part = sum_of((first, *turns(rest, 2, 8)))
-    part, to_y = together(part, to_y)
     got = [swap(part, "gy", 8, d) for d in (1, 2, 3)]
-    joined = call(
-        join_kernel, shape((3, 16, 192), BF), (to_y, got_x), (VM, VM),
-        [pltpu.VMEM((16, 192), F32)], 0, 2,
-    )
-    got_y = step(joined, "gy", 1)
     part = sum_of((part, *got))
     part, local = together(part, local)
     other = swap(part, "gy", 8, 4)

time: 77.9 us -> 73.4 us (0.942)
  starting transfers between devices: 36.8 us -> 32.2 us
    ppermute x5, starting transfers between devices: 14.3 us -> 9.07 us  [swap(): return lax.ppermute(value, axis, [(i, i ^ bits) for i in range(size)])]
    ppermute x5, waiting for transfers between devices: 3.15 us -> 6.06 us  [swap(): return lax.ppermute(value, axis, [(i, i ^ bits) for i in range(size)])]
    ppermute x1, starting transfers between devices: 1.92 us -> 3.63 us  [shards(): cot_xy = lax.ppermute(edge, ('gx', 'gy'), route)]
    ppermute x1, waiting for transfers between devices: 1.34 us -> 0.01 us  [shards(): cot_xy = lax.ppermute(edge, ('gx', 'gy'), route)]
    ppermute x4, starting transfers between devices: 11.3 us -> 10.2 us  [step(): return lax.ppermute(value, axis, route)]
    ppermute x6, waiting for transfers between devices: 8.6 us -> 7.79 us  [turns(): got[d] = lax.ppermute(parts[d - 1], 'gx', route)]
  transfers between devices with their start and end apart: 16 -> 16, of which waited for: 10 -> 8; matrix products, arithmetic and copies ran while one was open for 0% -> 0% of each run, Pallas kernels for 11% -> 12%
where the time goes in v2:
time: 73.4 us; the launch traced here: 73 us
  starting transfers between devices  32.2 us (44%)
  waiting for transfers between devices  26.4 us (36%)
  Pallas kernels  13.6 us (19%)
  between operations  0.78 us (1%)
    pallas_call x12, Pallas kernels, call(): pl.pallas_call(kernel, out_shape=outs, in_specs=[pl.BlockSpec(memory_spac...  13.6 us
    ppermute x4, waiting for transfers between devices, step(): return lax.ppermute(value, axis, route)  12.6 us
    ppermute x4, starting transfers between devices, step(): return lax.ppermute(value, axis, route)  10.2 us
    ppermute x6, starting transfers between devices, turns(): got[d] = lax.ppermute(parts[d - 1], 'gx', route)  9.32 us
    ppermute x5, starting transfers between devices, swap(): return lax.ppermute(value, axis, [(i, i ^ bits) for i in range(size)])  9.07 us
    ppermute x6, waiting for transfers between devices, turns(): got[d] = lax.ppermute(parts[d - 1], 'gx', route)  7.79 us
    ppermute x5, waiting for transfers between devices, swap(): return lax.ppermute(value, axis, [(i, i ^ bits) for i in range(size)])  6.06 us
    ppermute x1, starting transfers between devices, shards(): cot_xy = lax.ppermute(edge, ('gx', 'gy'), route)  3.63 us
  transfers between devices with their start and end apart: 16, of which 8 were waited for; matrix products, arithmetic and copies ran while one was open for 0% of the time, Pallas kernels for 12%

profile of v2, /device:TPU:224, one launch (start us, length us, event | category | flops | bytes accessed | tf_op | source)
XLA Modules:
  0.0 73.0 jit_solution(804518642936607003)
XLA Ops:
  0.6 1.0 %shard_map.103 = (bf16[3,64,192]{2,1,0:T(8,128)(2,1)S(1)}, bf16[3,16,192]{2,1,0:T(8,128)(2,1)S(1)}, bf16[3,16,192]{2,1,0:T(8,128)(2,1)S(1)}, bf16[3,8,192]{2,1,0:T(8,128)(2,1)S(1)}) custom-call(s32[1,1,3]{2,1,0:T(1,128)} %valid_in.7, bf16[1,1,3,64,192]{4,3,2,1,0:T(8,128)(2,1)} %cot_in.1), custom_call_target="tpu_custom_call" | custom-call | bytes 73740 | tf_op jit(solution)/shard_map/pallas_call | solution.py:39
  1.6 3.6 %collective-permute-start.2 = (bf16[3,8,192]{2,1,0:T(8,128)(2,1)S(1)}, bf16[3,8,192]{2,1,0:T(8,128)(2,1)S(1)}, u32[]{:S(2)}, u32[]{:S(2)}) collective-permute-start(bf16[3,8,192]{2,1,0:T(8,128)(2,1)S(1)} %get-tuple-element.45), channel_id=1, source_target_pairs={{9,0},{10,1},{11,2},{12,3},{13,4},{14,5},{15,6},{17,8},{18,9},{19,... | collective-permute-start | bytes 27656 | tf_op jit(solution)/shard_map/ppermute | solution.py:423
  5.3 3.7 %collective-permute-start = (bf16[3,16,192]{2,1,0:T(8,128)(2,1)S(1)}, bf16[3,16,192]{2,1,0:T(8,128)(2,1)S(1)}, u32[]{:S(2)}, u32[]{:S(2)}) collective-permute-start(bf16[3,16,192]{2,1,0:T(8,128)(2,1)S(1)} %get-tuple-element.54), channel_id=1, source_target_pairs={{8,0},{16,8},{24,16},{32,24},{40,32},{48,40},{56,48},{64,56},{72,6... | collective-permute-start | bytes 55304 | tf_op jit(solution)/shard_map/ppermute | solution.py:347
  8.9 2.7 %collective-permute-start.1 = (bf16[3,16,192]{2,1,0:T(8,128)(2,1)S(1)}, bf16[3,16,192]{2,1,0:T(8,128)(2,1)S(1)}, u32[]{:S(2)}, u32[]{:S(2)}) collective-permute-start(bf16[3,16,192]{2,1,0:T(8,128)(2,1)S(1)} %get-tuple-element.55), channel_id=1, source_target_pairs={{1,0},{2,1},{3,2},{4,3},{5,4},{6,5},{7,6},{9,8},{10,9},{11,10},{12... | collective-permute-start | bytes 55304 | tf_op jit(solution)/shard_map/ppermute | solution.py:347
  11.7 1.8 %shard_map.104 = (bf16[8,192,192]{2,1,0:T(8,128)(2,1)S(1)}, bf16[192,5184]{1,0:T(8,128)(2,1)S(1)}) custom-call(s32[1,1,3]{2,1,0:T(1,128)} %valid_in.7, bf16[1,1,3,192,512]{4,3,2,1,0:T(8,128)(2,1)} %bitcast.6, bf16[192,5184]{1,0:T(8,128)(2,1)} %bitcast.5), custom_call_target="tpu_custom_call" | custom-call | flops 382205952 | bytes 2580492 | tf_op jit(solution)/shard_map/pallas_call | solution.py:39
  13.5 2.1 %shard_map.105 = (f32[3,64,192]{2,1,0:T(8,128)S(1)}, bf16[3,32,192]{2,1,0:T(8,128)(2,1)S(1)}, f32[3,16,192]{2,1,0:T(8,128)S(1)}) custom-call(s32[1,1,2,12]{3,2,1,0:T(2,128)} %lrules_in.3, s32[1,1,12]{2,1,0:T(1,128)} %lcodes_in.3, s32[1,1,3,2,3]{4,3,2,1,0:T(2,128)} %bitcast.8, s32[1,3,1,3]{3,2,1,0:T(1,128)} %bitcast.10, ...), custom_call_target="tpu_custom_call" | custom-call | flops 382205952 | bytes 2580732 | tf_op jit(solution)/shard_map/pallas_call | solution.py:39
  15.6 2.6 %shard_map.106 = (f32[4096,128]{1,0:T(8,128)S(1)}, bf16[4096,128]{1,0:T(8,128)(2,1)S(1)}, bf16[8,192,192]{2,1,0:T(8,128)(2,1)S(1)}) custom-call(s32[1,1,2,12]{3,2,1,0:T(2,128)} %lrules_in.3, s32[1,1,12]{2,1,0:T(1,128)} %lcodes_in.3, s32[1,1,3,2,3]{4,3,2,1,0:T(2,128)} %bitcast.9, s32[1,3,1,3]{3,2,1,0:T(1,128)} %bitcast.11, ...), custom_call_target="tpu_custom_call" | custom-call | flops 382205952 | bytes 709884 | tf_op jit(solution)/shard_map/pallas_call | solution.py:39
  18.2 0.1 collective-permute-start.3
  18.4 2.6 %collective-permute-done.3.refs_0_ = bf16[4096,128]{1,0:T(8,128)(2,1)S(1)} collective-permute-done((bf16[4096,128]{1,0:T(8,128)(2,1)S(1)}, bf16[4096,128]{1,0:T(8,128)(2,1)S(1)}, u32[]{:S(2)}, u32[]{:S(2)}) %collective-permute-start.3) | collective-permute-done | bytes 1048608 | tf_op jit(solution)/shard_map/ppermute | solution.py:341
  21.0 0.2 shard_map.107
  21.2 1.7 %collective-permute-start.4 = (bf16[1024,128]{1,0:T(8,128)(2,1)S(1)}, bf16[1024,128]{1,0:T(8,128)(2,1)S(1)}, u32[]{:S(2)}, u32[]{:S(2)}) collective-permute-start(bf16[1024,128]{1,0:T(8,128)(2,1)S(1)} %get-tuple-element.65), channel_id=1, source_target_pairs={{0,64},{8,24},{16,80},{24,8},{32,96},{40,56},{48,112},{56,40},{64,... | collective-permute-start | bytes 786440 | tf_op jit(solution)/shard_map/ppermute | solution.py:386
  22.8 2.9 %collective-permute-start.5 = (bf16[1024,128]{1,0:T(8,128)(2,1)S(1)}, bf16[1024,128]{1,0:T(8,128)(2,1)S(1)}, u32[]{:S(2)}, u32[]{:S(2)}) collective-permute-start(bf16[1024,128]{1,0:T(8,128)(2,1)S(1)} %get-tuple-element.66), channel_id=1, source_target_pairs={{0,128},{8,40},{16,144},{24,56},{32,160},{40,8},{48,176},{56,24},{... | collective-permute-start | bytes 786440 | tf_op jit(solution)/shard_map/ppermute | solution.py:386
  25.8 0.2 collective-permute-start.6
  26.0 1.9 %collective-permute-start.7 = (bf16[3,32,192]{2,1,0:T(8,128)(2,1)S(1)}, bf16[3,32,192]{2,1,0:T(8,128)(2,1)S(1)}, u32[]{:S(2)}, u32[]{:S(2)}) collective-permute-start(bf16[3,32,192]{2,1,0:T(8,128)(2,1)S(1)} %get-tuple-element.69), channel_id=1, source_target_pairs={{0,8},{8,16},{16,24},{24,32},{32,40},{40,48},{48,56},{56,64},{64,7... | collective-permute-start | bytes 110600 | tf_op jit(solution)/shard_map/ppermute | solution.py:347
  27.9 3.4 %shard_map.108 = bf16[1,1,3,192,512]{4,3,2,1,0:T(8,128)(2,1)} custom-call(s32[1,1,3]{2,1,0:T(1,128)} %valid_in.7, bf16[8,192,192]{2,1,0:T(8,128)(2,1)S(1)} %get-tuple-element.68.shifts, bf16[192,5184]{1,0:T(8,128)(2,1)S(1)} %get-tuple-element.48.weight), custom_call_target="tpu_custom_call" | custom-call | flops 382205952 | bytes 2580492 | tf_op jit(solution)/shard_map/pallas_call | solution.py:39
  31.2 2.8 %collective-permute-done.7.got_x = bf16[3,32,192]{2,1,0:T(8,128)(2,1)S(1)} collective-permute-done((bf16[3,32,192]{2,1,0:T(8,128)(2,1)S(1)}, bf16[3,32,192]{2,1,0:T(8,128)(2,1)S(1)}, u32[]{:S(2)}, u32[]{:S(2)}) %collective-permute-start.7) | collective-permute-done | bytes 36896 | tf_op jit(solution)/shard_map/ppermute | solution.py:347
  34.0 1.7 %collective-permute-done.6.refs_2_ = bf16[1024,128]{1,0:T(8,128)(2,1)S(1)} collective-permute-done((bf16[1024,128]{1,0:T(8,128)(2,1)S(1)}, bf16[1024,128]{1,0:T(8,128)(2,1)S(1)}, u32[]{:S(2)}, u32[]{:S(2)}) %collective-permute-start.6) | collective-permute-done | bytes 262176 | tf_op jit(solution)/shard_map/ppermute | solution.py:386
  35.7 0.1 shard_map.109
  35.8 1.8 %collective-permute-start.8 = (bf16[256,128]{1,0:T(8,128)(2,1)S(1)}, bf16[256,128]{1,0:T(8,128)(2,1)S(1)}, u32[]{:S(2)}, u32[]{:S(2)}) collective-permute-start(bf16[256,128]{1,0:T(8,128)(2,1)S(1)} %get-tuple-element.76), channel_id=1, source_target_pairs={{0,16},{8,72},{16,0},{24,88},{32,48},{40,104},{48,32},{56,120},{64... | collective-permute-start | bytes 196616 | tf_op jit(solution)/shard_map/ppermute | solution.py:386
  37.6 2.8 %collective-permute-start.9 = (bf16[256,128]{1,0:T(8,128)(2,1)S(1)}, bf16[256,128]{1,0:T(8,128)(2,1)S(1)}, u32[]{:S(2)}, u32[]{:S(2)}) collective-permute-start(bf16[256,128]{1,0:T(8,128)(2,1)S(1)} %get-tuple-element.77), channel_id=1, source_target_pairs={{0,32},{8,136},{16,48},{24,152},{32,0},{40,168},{48,16},{56,184},{... | collective-permute-start | bytes 196616 | tf_op jit(solution)/shard_map/ppermute | solution.py:386
  40.4 3.1 %collective-permute-done.9.two = bf16[256,128]{1,0:T(8,128)(2,1)S(1)} collective-permute-done((bf16[256,128]{1,0:T(8,128)(2,1)S(1)}, bf16[256,128]{1,0:T(8,128)(2,1)S(1)}, u32[]{:S(2)}, u32[]{:S(2)}) %collective-permute-start.9) | collective-permute-done | bytes 65568 | tf_op jit(solution)/shard_map/ppermute | solution.py:386
  43.5 3.0 %collective-permute-done.10.three = bf16[256,128]{1,0:T(8,128)(2,1)S(1)} collective-permute-done((bf16[256,128]{1,0:T(8,128)(2,1)S(1)}, bf16[256,128]{1,0:T(8,128)(2,1)S(1)}, u32[]{:S(2)}, u32[]{:S(2)}) %collective-permute-start.10) | collective-permute-done | bytes 65568 | tf_op jit(solution)/shard_map/ppermute | solution.py:386
  46.5 0.1 collective-permute-start.13
  46.6 3.2 %collective-permute-start.12 = (bf16[256,128]{1,0:T(8,128)(2,1)S(1)}, bf16[256,128]{1,0:T(8,128)(2,1)S(1)}, u32[]{:S(2)}, u32[]{:S(2)}) collective-permute-start(bf16[256,128]{1,0:T(8,128)(2,1)S(1)} %shard_map.110.first), channel_id=1, source_target_pairs={{0,2},{1,3},{2,0},{3,1},{4,6},{5,7},{6,4},{7,5},{8,10},{9,11},{10,... | collective-permute-start | bytes 196616 | tf_op jit(solution)/shard_map/ppermute | solution.py:341
  49.8 0.8 %collective-permute-start.11 = (bf16[256,128]{1,0:T(8,128)(2,1)S(1)}, bf16[256,128]{1,0:T(8,128)(2,1)S(1)}, u32[]{:S(2)}, u32[]{:S(2)}) collective-permute-start(bf16[256,128]{1,0:T(8,128)(2,1)S(1)} %shard_map.110.first), channel_id=1, source_target_pairs={{0,1},{1,0},{2,3},{3,2},{4,5},{5,4},{6,7},{7,6},{8,9},{9,8},{10,11... | collective-permute-start | bytes 196616 | tf_op jit(solution)/shard_map/ppermute | solution.py:341
  50.7 2.1 %collective-permute-done.13.three = bf16[256,128]{1,0:T(8,128)(2,1)S(1)} collective-permute-done((bf16[256,128]{1,0:T(8,128)(2,1)S(1)}, bf16[256,128]{1,0:T(8,128)(2,1)S(1)}, u32[]{:S(2)}, u32[]{:S(2)}) %collective-permute-start.13) | collective-permute-done | bytes 65568 | tf_op jit(solution)/shard_map/ppermute | solution.py:341
  52.7 1.3 %collective-permute-done.11.one = bf16[256,128]{1,0:T(8,128)(2,1)S(1)} collective-permute-done((bf16[256,128]{1,0:T(8,128)(2,1)S(1)}, bf16[256,128]{1,0:T(8,128)(2,1)S(1)}, u32[]{:S(2)}, u32[]{:S(2)}) %collective-permute-start.11) | collective-permute-done | bytes 65568 | tf_op jit(solution)/shard_map/ppermute | solution.py:341
  54.1 4.8 %collective-permute-start.14 = (bf16[256,128]{1,0:T(8,128)(2,1)S(1)}, bf16[256,128]{1,0:T(8,128)(2,1)S(1)}, u32[]{:S(2)}, u32[]{:S(2)}) collective-permute-start(bf16[256,128]{1,0:T(8,128)(2,1)S(1)} %shard_map.111.mine), channel_id=1, source_target_pairs={{0,4},{1,5},{2,6},{3,7},{4,0},{5,1},{6,2},{7,3},{8,12},{9,13},{10,... | collective-permute-start | bytes 196616 | tf_op jit(solution)/shard_map/ppermute | solution.py:341
  58.9 1.9 %collective-permute-start.15 = (bf16[3,16,192]{2,1,0:T(8,128)(2,1)S(1)}, bf16[3,16,192]{2,1,0:T(8,128)(2,1)S(1)}, u32[]{:S(2)}, u32[]{:S(2)}) collective-permute-start(bf16[3,16,192]{2,1,0:T(8,128)(2,1)S(1)} %shard_map.112), channel_id=1, source_target_pairs={{0,1},{1,2},{2,3},{3,4},{4,5},{5,6},{6,7},{8,9},{9,10},{10,11},{11... | collective-permute-start | bytes 55304 | tf_op jit(solution)/shard_map/ppermute | solution.py:347
  60.9 9.8 %collective-permute-done.15.got_y = bf16[3,16,192]{2,1,0:T(8,128)(2,1)S(1)} collective-permute-done((bf16[3,16,192]{2,1,0:T(8,128)(2,1)S(1)}, bf16[3,16,192]{2,1,0:T(8,128)(2,1)S(1)}, u32[]{:S(2)}, u32[]{:S(2)}) %collective-permute-start.15) | collective-permute-done | bytes 18464 | tf_op jit(solution)/shard_map/ppermute | solution.py:347
  70.7 1.5 %shard_map.113 = bf16[1,1,3,64,192]{4,3,2,1,0:T(8,128)(2,1)} custom-call(s32[1,1,3]{2,1,0:T(1,128)} %valid_in.7, f32[3,64,192]{2,1,0:T(8,128)S(1)} %get-tuple-element.81.local, bf16[3,32,192]{2,1,0:T(8,128)(2,1)S(1)} %collective-permute-done.7.got_x, bf16[3,16,192]{2,1,0:T(8,128)(2,1)S(1)} %collective-permute-done.15.got_y), custom_call_target="tpu_custom_call" | custom-call | bytes 202764 | tf_op jit(solution)/shard_map/pallas_call | solution.py:39
  72.2 0.8 %shard_map.114 = f32[162,192]{1,0:T(8,128)} custom-call(bf16[256,128]{1,0:T(8,128)(2,1)S(1)} %shard_map.111.mine, bf16[256,128]{1,0:T(8,128)(2,1)S(1)} %collective-permute-done.14.other), custom_call_target="tpu_custom_call" | custom-call | bytes 131072 | tf_op jit(solution)/shard_map/pallas_call | solution.py:39
  (12 shorter events, 0.1 us)
Async XLA Ops:
  1.6 14.0 %collective-permute-start.2 = (bf16[3,8,192]{2,1,0:T(8,128)(2,1)S(1)}, bf16[3,8,192]{2,1,0:T(8,128)(2,1)S(1)}, u32[]{:S(2)}, u32[]{:S(2)}) collective-permute-start(bf16[3,8,192]{2,1,0:T(8,128)(2,1)S(1)} %get-tuple-element.45), channel_id=1, source_target_pairs={{9,0},{10,1},{11,2},{12,3},{13,4},{14,5},{15,6},{17,8},{18,9},{19,... | collective-permute-start | bytes 27656 | tf_op jit(solution)/shard_map/ppermute | solution.py:423
  5.3 10.3 %collective-permute-start = (bf16[3,16,192]{2,1,0:T(8,128)(2,1)S(1)}, bf16[3,16,192]{2,1,0:T(8,128)(2,1)S(1)}, u32[]{:S(2)}, u32[]{:S(2)}) collective-permute-start(bf16[3,16,192]{2,1,0:T(8,128)(2,1)S(1)} %get-tuple-element.54), channel_id=1, source_target_pairs={{8,0},{16,8},{24,16},{32,24},{40,32},{48,40},{56,48},{64,56},{72,6... | collective-permute-start | bytes 55304 | tf_op jit(solution)/shard_map/ppermute | solution.py:347
  8.9 6.7 %collective-permute-start.1 = (bf16[3,16,192]{2,1,0:T(8,128)(2,1)S(1)}, bf16[3,16,192]{2,1,0:T(8,128)(2,1)S(1)}, u32[]{:S(2)}, u32[]{:S(2)}) collective-permute-start(bf16[3,16,192]{2,1,0:T(8,128)(2,1)S(1)} %get-tuple-element.55), channel_id=1, source_target_pairs={{1,0},{2,1},{3,2},{4,3},{5,4},{6,5},{7,6},{9,8},{10,9},{11,10},{12... | collective-permute-start | bytes 55304 | tf_op jit(solution)/shard_map/ppermute | solution.py:347
  18.2 2.7 %collective-permute-start.3 = (bf16[4096,128]{1,0:T(8,128)(2,1)S(1)}, bf16[4096,128]{1,0:T(8,128)(2,1)S(1)}, u32[]{:S(2)}, u32[]{:S(2)}) collective-permute-start(bf16[4096,128]{1,0:T(8,128)(2,1)S(1)} %get-tuple-element.59), channel_id=1, source_target_pairs={{0,8},{8,0},{16,24},{24,16},{32,40},{40,32},{48,56},{56,48},{64,72... | collective-permute-start | bytes 3145736 | tf_op jit(solution)/shard_map/ppermute | solution.py:341
  21.2 12.8 %collective-permute-start.4 = (bf16[1024,128]{1,0:T(8,128)(2,1)S(1)}, bf16[1024,128]{1,0:T(8,128)(2,1)S(1)}, u32[]{:S(2)}, u32[]{:S(2)}) collective-permute-start(bf16[1024,128]{1,0:T(8,128)(2,1)S(1)} %get-tuple-element.65), channel_id=1, source_target_pairs={{0,64},{8,24},{16,80},{24,8},{32,96},{40,56},{48,112},{56,40},{64,... | collective-permute-start | bytes 786440 | tf_op jit(solution)/shard_map/ppermute | solution.py:386
  22.8 11.2 %collective-permute-start.5 = (bf16[1024,128]{1,0:T(8,128)(2,1)S(1)}, bf16[1024,128]{1,0:T(8,128)(2,1)S(1)}, u32[]{:S(2)}, u32[]{:S(2)}) collective-permute-start(bf16[1024,128]{1,0:T(8,128)(2,1)S(1)} %get-tuple-element.66), channel_id=1, source_target_pairs={{0,128},{8,40},{16,144},{24,56},{32,160},{40,8},{48,176},{56,24},{... | collective-permute-start | bytes 786440 | tf_op jit(solution)/shard_map/ppermute | solution.py:386
  25.8 10.0 %collective-permute-start.6 = (bf16[1024,128]{1,0:T(8,128)(2,1)S(1)}, bf16[1024,128]{1,0:T(8,128)(2,1)S(1)}, u32[]{:S(2)}, u32[]{:S(2)}) collective-permute-start(bf16[1024,128]{1,0:T(8,128)(2,1)S(1)} %get-tuple-element.67), channel_id=1, source_target_pairs={{0,192},{8,56},{16,208},{24,40},{32,224},{40,24},{48,240},{56,8},{... | collective-permute-start | bytes 786440 | tf_op jit(solution)/shard_map/ppermute | solution.py:386
  26.0 8.0 %collective-permute-start.7 = (bf16[3,32,192]{2,1,0:T(8,128)(2,1)S(1)}, bf16[3,32,192]{2,1,0:T(8,128)(2,1)S(1)}, u32[]{:S(2)}, u32[]{:S(2)}) collective-permute-start(bf16[3,32,192]{2,1,0:T(8,128)(2,1)S(1)} %get-tuple-element.69), channel_id=1, source_target_pairs={{0,8},{8,16},{16,24},{24,32},{32,40},{40,48},{48,56},{56,64},{64,7... | collective-permute-start | bytes 110600 | tf_op jit(solution)/shard_map/ppermute | solution.py:347
  35.8 4.5 %collective-permute-start.8 = (bf16[256,128]{1,0:T(8,128)(2,1)S(1)}, bf16[256,128]{1,0:T(8,128)(2,1)S(1)}, u32[]{:S(2)}, u32[]{:S(2)}) collective-permute-start(bf16[256,128]{1,0:T(8,128)(2,1)S(1)} %get-tuple-element.76), channel_id=1, source_target_pairs={{0,16},{8,72},{16,0},{24,88},{32,48},{40,104},{48,32},{56,120},{64... | collective-permute-start | bytes 196616 | tf_op jit(solution)/shard_map/ppermute | solution.py:386
  37.6 5.8 %collective-permute-start.9 = (bf16[256,128]{1,0:T(8,128)(2,1)S(1)}, bf16[256,128]{1,0:T(8,128)(2,1)S(1)}, u32[]{:S(2)}, u32[]{:S(2)}) collective-permute-start(bf16[256,128]{1,0:T(8,128)(2,1)S(1)} %get-tuple-element.77), channel_id=1, source_target_pairs={{0,32},{8,136},{16,48},{24,152},{32,0},{40,168},{48,16},{56,184},{... | collective-permute-start | bytes 196616 | tf_op jit(solution)/shard_map/ppermute | solution.py:386
  40.4 6.1 %collective-permute-start.10 = (bf16[256,128]{1,0:T(8,128)(2,1)S(1)}, bf16[256,128]{1,0:T(8,128)(2,1)S(1)}, u32[]{:S(2)}, u32[]{:S(2)}) collective-permute-start(bf16[256,128]{1,0:T(8,128)(2,1)S(1)} %get-tuple-element.78), channel_id=1, source_target_pairs={{0,48},{8,200},{16,32},{24,216},{32,16},{40,232},{48,0},{56,248},{... | collective-permute-start | bytes 196616 | tf_op jit(solution)/shard_map/ppermute | solution.py:386
  46.5 6.3 %collective-permute-start.13 = (bf16[256,128]{1,0:T(8,128)(2,1)S(1)}, bf16[256,128]{1,0:T(8,128)(2,1)S(1)}, u32[]{:S(2)}, u32[]{:S(2)}) collective-permute-start(bf16[256,128]{1,0:T(8,128)(2,1)S(1)} %shard_map.110.first), channel_id=1, source_target_pairs={{0,3},{1,2},{2,1},{3,0},{4,7},{5,6},{6,5},{7,4},{8,11},{9,10},{10,... | collective-permute-start | bytes 196616 | tf_op jit(solution)/shard_map/ppermute | solution.py:341
  46.6 6.2 %collective-permute-start.12 = (bf16[256,128]{1,0:T(8,128)(2,1)S(1)}, bf16[256,128]{1,0:T(8,128)(2,1)S(1)}, u32[]{:S(2)}, u32[]{:S(2)}) collective-permute-start(bf16[256,128]{1,0:T(8,128)(2,1)S(1)} %shard_map.110.first), channel_id=1, source_target_pairs={{0,2},{1,3},{2,0},{3,1},{4,6},{5,7},{6,4},{7,5},{8,10},{9,11},{10,... | collective-permute-start | bytes 196616 | tf_op jit(solution)/shard_map/ppermute | solution.py:341
  49.8 4.3 %collective-permute-start.11 = (bf16[256,128]{1,0:T(8,128)(2,1)S(1)}, bf16[256,128]{1,0:T(8,128)(2,1)S(1)}, u32[]{:S(2)}, u32[]{:S(2)}) collective-permute-start(bf16[256,128]{1,0:T(8,128)(2,1)S(1)} %shard_map.110.first), channel_id=1, source_target_pairs={{0,1},{1,0},{2,3},{3,2},{4,5},{5,4},{6,7},{7,6},{8,9},{9,8},{10,11... | collective-permute-start | bytes 196616 | tf_op jit(solution)/shard_map/ppermute | solution.py:341
  54.1 18.1 %collective-permute-start.14 = (bf16[256,128]{1,0:T(8,128)(2,1)S(1)}, bf16[256,128]{1,0:T(8,128)(2,1)S(1)}, u32[]{:S(2)}, u32[]{:S(2)}) collective-permute-start(bf16[256,128]{1,0:T(8,128)(2,1)S(1)} %shard_map.111.mine), channel_id=1, source_target_pairs={{0,4},{1,5},{2,6},{3,7},{4,0},{5,1},{6,2},{7,3},{8,12},{9,13},{10,... | collective-permute-start | bytes 196616 | tf_op jit(solution)/shard_map/ppermute | solution.py:341
  58.9 11.7 %collective-permute-start.15 = (bf16[3,16,192]{2,1,0:T(8,128)(2,1)S(1)}, bf16[3,16,192]{2,1,0:T(8,128)(2,1)S(1)}, u32[]{:S(2)}, u32[]{:S(2)}) collective-permute-start(bf16[3,16,192]{2,1,0:T(8,128)(2,1)S(1)} %shard_map.112), channel_id=1, source_target_pairs={{0,1},{1,2},{2,3},{3,4},{4,5},{5,6},{6,7},{8,9},{9,10},{10,11},{11... | collective-permute-start | bytes 55304 | tf_op jit(solution)/shard_map/ppermute | solution.py:347

commit v3 on v2

--- a/solution.py
+++ b/solution.py
@@ -454,12 +454,11 @@
         flops,
         18,
     )
-    send, to_x = together(send, to_x)
     arrived = swap(send, "gx", 32, 1)
+    first, rest = split_sum(keep, [arrived], 8)
+    rest, shifts, to_x = together(rest, shifts, to_x)
+    arrived = turns(rest, 8, 2)
     got_x = step(to_x, "gx", 1)
-    first, rest = split_sum(keep, [arrived], 8)
-    rest, shifts = together(rest, shifts)
-    arrived = turns(rest, 8, 2)
     features_grad = call(
         features_kernel,
         shape((1, 1, 3, 192, 512), BF),
@@ -469,16 +468,16 @@
         flops,
         12,
     )
-    features_grad, got_x, to_y = together(features_grad, got_x, to_y)
+    arrived, features_grad = together(arrived, features_grad)
+    first, rest = split_sum(first, arrived, 4)
+    part = sum_of((first, *turns(rest, 2, 8)))
+    part, to_y = together(part, to_y)
+    got = [swap(part, "gy", 8, d) for d in (1, 2, 3)]
     joined = call(
         join_kernel, shape((3, 16, 192), BF), (to_y, got_x), (VM, VM),
         [pltpu.VMEM((16, 192), F32)], 0, 2,
     )
     got_y = step(joined, "gy", 1)
-    arrived, features_grad = together(arrived, features_grad)
-    first, rest = split_sum(first, arrived, 4)
-    part = sum_of((first, *turns(rest, 2, 8)))
-    got = [swap(part, "gy", 8, d) for d in (1, 2, 3)]
     part = sum_of((part, *got))
     part, local = together(part, local)
     other = swap(part, "gy", 8, 4)

time: 73.4 us -> 78.8 us (1.074)
  waiting for transfers between devices: 26.4 us -> 31.8 us
    ppermute x6, waiting for transfers between devices: 7.79 us -> 12.5 us  [turns(): got[d] = lax.ppermute(parts[d - 1], 'gx', route)]
  transfers between devices with their start and end apart: 16 -> 16, of which waited for: 8 -> 9; matrix products, arithmetic and copies ran while one was open for 0% -> 0% of each run, Pallas kernels for 12% -> 11%
where the time goes in v3:
time: 78.8 us; the launch traced here: 78.4 us
  starting transfers between devices  32.2 us (41%)
  waiting for transfers between devices  31.8 us (40%)
  Pallas kernels  13.6 us (17%)
  between operations  0.79 us (1%)
    pallas_call x12, Pallas kernels, call(): pl.pallas_call(kernel, out_shape=outs, in_specs=[pl.BlockSpec(memory_spac...  13.6 us
    ppermute x4, waiting for transfers between devices, step(): return lax.ppermute(value, axis, route)  13.3 us
    ppermute x6, waiting for transfers between devices, turns(): got[d] = lax.ppermute(parts[d - 1], 'gx', route)  12.5 us
    ppermute x4, starting transfers between devices, step(): return lax.ppermute(value, axis, route)  10.2 us
    ppermute x6, starting transfers between devices, turns(): got[d] = lax.ppermute(parts[d - 1], 'gx', route)  9.32 us
    ppermute x5, starting transfers between devices, swap(): return lax.ppermute(value, axis, [(i, i ^ bits) for i in range(size)])  9.07 us
    ppermute x5, waiting for transfers between devices, swap(): return lax.ppermute(value, axis, [(i, i ^ bits) for i in range(size)])  6.06 us
    ppermute x1, starting transfers between devices, shards(): cot_xy = lax.ppermute(edge, ('gx', 'gy'), route)  3.63 us
  transfers between devices with their start and end apart: 16, of which 9 were waited for; matrix products, arithmetic and copies ran while one was open for 0% of the time, Pallas kernels for 11%

profile of v3, /device:TPU:224, one launch (start us, length us, event | category | flops | bytes accessed | tf_op | source)
XLA Modules:
  0.0 78.4 jit_solution(17367881059912418961)
XLA Ops:
  0.6 1.0 %shard_map.103 = (bf16[3,64,192]{2,1,0:T(8,128)(2,1)S(1)}, bf16[3,16,192]{2,1,0:T(8,128)(2,1)S(1)}, bf16[3,16,192]{2,1,0:T(8,128)(2,1)S(1)}, bf16[3,8,192]{2,1,0:T(8,128)(2,1)S(1)}) custom-call(s32[1,1,3]{2,1,0:T(1,128)} %valid_in.7, bf16[1,1,3,64,192]{4,3,2,1,0:T(8,128)(2,1)} %cot_in.1), custom_call_target="tpu_custom_call" | custom-call | bytes 73740 | tf_op jit(solution)/shard_map/pallas_call | solution.py:39
  1.6 3.6 %collective-permute-start.2 = (bf16[3,8,192]{2,1,0:T(8,128)(2,1)S(1)}, bf16[3,8,192]{2,1,0:T(8,128)(2,1)S(1)}, u32[]{:S(2)}, u32[]{:S(2)}) collective-permute-start(bf16[3,8,192]{2,1,0:T(8,128)(2,1)S(1)} %get-tuple-element.43), channel_id=1, source_target_pairs={{9,0},{10,1},{11,2},{12,3},{13,4},{14,5},{15,6},{17,8},{18,9},{19,... | collective-permute-start | bytes 27656 | tf_op jit(solution)/shard_map/ppermute | solution.py:423
  5.3 3.7 %collective-permute-start = (bf16[3,16,192]{2,1,0:T(8,128)(2,1)S(1)}, bf16[3,16,192]{2,1,0:T(8,128)(2,1)S(1)}, u32[]{:S(2)}, u32[]{:S(2)}) collective-permute-start(bf16[3,16,192]{2,1,0:T(8,128)(2,1)S(1)} %get-tuple-element.52), channel_id=1, source_target_pairs={{8,0},{16,8},{24,16},{32,24},{40,32},{48,40},{56,48},{64,56},{72,6... | collective-permute-start | bytes 55304 | tf_op jit(solution)/shard_map/ppermute | solution.py:347
  8.9 2.7 %collective-permute-start.1 = (bf16[3,16,192]{2,1,0:T(8,128)(2,1)S(1)}, bf16[3,16,192]{2,1,0:T(8,128)(2,1)S(1)}, u32[]{:S(2)}, u32[]{:S(2)}) collective-permute-start(bf16[3,16,192]{2,1,0:T(8,128)(2,1)S(1)} %get-tuple-element.53), channel_id=1, source_target_pairs={{1,0},{2,1},{3,2},{4,3},{5,4},{6,5},{7,6},{9,8},{10,9},{11,10},{12... | collective-permute-start | bytes 55304 | tf_op jit(solution)/shard_map/ppermute | solution.py:347
  11.7 1.8 %shard_map.104 = (bf16[8,192,192]{2,1,0:T(8,128)(2,1)S(1)}, bf16[192,5184]{1,0:T(8,128)(2,1)S(1)}) custom-call(s32[1,1,3]{2,1,0:T(1,128)} %valid_in.7, bf16[1,1,3,192,512]{4,3,2,1,0:T(8,128)(2,1)} %bitcast.6, bf16[192,5184]{1,0:T(8,128)(2,1)} %bitcast.5), custom_call_target="tpu_custom_call" | custom-call | flops 382205952 | bytes 2580492 | tf_op jit(solution)/shard_map/pallas_call | solution.py:39
  13.5 2.1 %shard_map.105 = (f32[3,64,192]{2,1,0:T(8,128)S(1)}, bf16[3,32,192]{2,1,0:T(8,128)(2,1)S(1)}, f32[3,16,192]{2,1,0:T(8,128)S(1)}) custom-call(s32[1,1,2,12]{3,2,1,0:T(2,128)} %lrules_in.3, s32[1,1,12]{2,1,0:T(1,128)} %lcodes_in.3, s32[1,1,3,2,3]{4,3,2,1,0:T(2,128)} %bitcast.8, s32[1,3,1,3]{3,2,1,0:T(1,128)} %bitcast.10, ...), custom_call_target="tpu_custom_call" | custom-call | flops 382205952 | bytes 2580732 | tf_op jit(solution)/shard_map/pallas_call | solution.py:39
  15.6 2.6 %shard_map.106 = (f32[4096,128]{1,0:T(8,128)S(1)}, bf16[4096,128]{1,0:T(8,128)(2,1)S(1)}, bf16[8,192,192]{2,1,0:T(8,128)(2,1)S(1)}) custom-call(s32[1,1,2,12]{3,2,1,0:T(2,128)} %lrules_in.3, s32[1,1,12]{2,1,0:T(1,128)} %lcodes_in.3, s32[1,1,3,2,3]{4,3,2,1,0:T(2,128)} %bitcast.9, s32[1,3,1,3]{3,2,1,0:T(1,128)} %bitcast.11, ...), custom_call_target="tpu_custom_call" | custom-call | flops 382205952 | bytes 709884 | tf_op jit(solution)/shard_map/pallas_call | solution.py:39
  18.2 0.1 collective-permute-start.3
  18.4 2.6 %collective-permute-done.3.refs_0_ = bf16[4096,128]{1,0:T(8,128)(2,1)S(1)} collective-permute-done((bf16[4096,128]{1,0:T(8,128)(2,1)S(1)}, bf16[4096,128]{1,0:T(8,128)(2,1)S(1)}, u32[]{:S(2)}, u32[]{:S(2)}) %collective-permute-start.3) | collective-permute-done | bytes 1048608 | tf_op jit(solution)/shard_map/ppermute | solution.py:341
  21.0 0.2 shard_map.107
  21.2 1.7 %collective-permute-start.4 = (bf16[1024,128]{1,0:T(8,128)(2,1)S(1)}, bf16[1024,128]{1,0:T(8,128)(2,1)S(1)}, u32[]{:S(2)}, u32[]{:S(2)}) collective-permute-start(bf16[1024,128]{1,0:T(8,128)(2,1)S(1)} %get-tuple-element.62), channel_id=1, source_target_pairs={{0,64},{8,24},{16,80},{24,8},{32,96},{40,56},{48,112},{56,40},{64,... | collective-permute-start | bytes 786440 | tf_op jit(solution)/shard_map/ppermute | solution.py:386
  22.8 2.9 %collective-permute-start.5 = (bf16[1024,128]{1,0:T(8,128)(2,1)S(1)}, bf16[1024,128]{1,0:T(8,128)(2,1)S(1)}, u32[]{:S(2)}, u32[]{:S(2)}) collective-permute-start(bf16[1024,128]{1,0:T(8,128)(2,1)S(1)} %get-tuple-element.63), channel_id=1, source_target_pairs={{0,128},{8,40},{16,144},{24,56},{32,160},{40,8},{48,176},{56,24},{... | collective-permute-start | bytes 786440 | tf_op jit(solution)/shard_map/ppermute | solution.py:386
  25.8 0.2 collective-permute-start.6
  26.0 3.3 %shard_map.108 = bf16[1,1,3,192,512]{4,3,2,1,0:T(8,128)(2,1)} custom-call(s32[1,1,3]{2,1,0:T(1,128)} %valid_in.7, bf16[8,192,192]{2,1,0:T(8,128)(2,1)S(1)} %get-tuple-element.65.shifts, bf16[192,5184]{1,0:T(8,128)(2,1)S(1)} %get-tuple-element.46.weight), custom_call_target="tpu_custom_call" | custom-call | flops 382205952 | bytes 2580492 | tf_op jit(solution)/shard_map/pallas_call | solution.py:39
  29.3 3.7 %collective-permute-done.5.refs_1_ = bf16[1024,128]{1,0:T(8,128)(2,1)S(1)} collective-permute-done((bf16[1024,128]{1,0:T(8,128)(2,1)S(1)}, bf16[1024,128]{1,0:T(8,128)(2,1)S(1)}, u32[]{:S(2)}, u32[]{:S(2)}) %collective-permute-start.5) | collective-permute-done | bytes 262176 | tf_op jit(solution)/shard_map/ppermute | solution.py:386
  33.0 2.7 %collective-permute-done.6.refs_2_ = bf16[1024,128]{1,0:T(8,128)(2,1)S(1)} collective-permute-done((bf16[1024,128]{1,0:T(8,128)(2,1)S(1)}, bf16[1024,128]{1,0:T(8,128)(2,1)S(1)}, u32[]{:S(2)}, u32[]{:S(2)}) %collective-permute-start.6) | collective-permute-done | bytes 262176 | tf_op jit(solution)/shard_map/ppermute | solution.py:386
  35.7 0.1 shard_map.109
  35.8 0.2 collective-permute-start.7
  36.0 4.3 %collective-permute-start.8 = (bf16[256,128]{1,0:T(8,128)(2,1)S(1)}, bf16[256,128]{1,0:T(8,128)(2,1)S(1)}, u32[]{:S(2)}, u32[]{:S(2)}) collective-permute-start(bf16[256,128]{1,0:T(8,128)(2,1)S(1)} %get-tuple-element.71), channel_id=1, source_target_pairs={{0,32},{8,136},{16,48},{24,152},{32,0},{40,168},{48,16},{56,184},{... | collective-permute-start | bytes 196616 | tf_op jit(solution)/shard_map/ppermute | solution.py:386
  40.4 2.9 %collective-permute-done.8.two = bf16[256,128]{1,0:T(8,128)(2,1)S(1)} collective-permute-done((bf16[256,128]{1,0:T(8,128)(2,1)S(1)}, bf16[256,128]{1,0:T(8,128)(2,1)S(1)}, u32[]{:S(2)}, u32[]{:S(2)}) %collective-permute-start.8) | collective-permute-done | bytes 65568 | tf_op jit(solution)/shard_map/ppermute | solution.py:386
  43.3 3.1 %collective-permute-done.9.three = bf16[256,128]{1,0:T(8,128)(2,1)S(1)} collective-permute-done((bf16[256,128]{1,0:T(8,128)(2,1)S(1)}, bf16[256,128]{1,0:T(8,128)(2,1)S(1)}, u32[]{:S(2)}, u32[]{:S(2)}) %collective-permute-start.9) | collective-permute-done | bytes 65568 | tf_op jit(solution)/shard_map/ppermute | solution.py:386
  46.6 3.2 %collective-permute-start.11 = (bf16[256,128]{1,0:T(8,128)(2,1)S(1)}, bf16[256,128]{1,0:T(8,128)(2,1)S(1)}, u32[]{:S(2)}, u32[]{:S(2)}) collective-permute-start(bf16[256,128]{1,0:T(8,128)(2,1)S(1)} %shard_map.110.first), channel_id=1, source_target_pairs={{0,2},{1,3},{2,0},{3,1},{4,6},{5,7},{6,4},{7,5},{8,10},{9,11},{10,... | collective-permute-start | bytes 196616 | tf_op jit(solution)/shard_map/ppermute | solution.py:341
  49.8 0.8 %collective-permute-start.10 = (bf16[256,128]{1,0:T(8,128)(2,1)S(1)}, bf16[256,128]{1,0:T(8,128)(2,1)S(1)}, u32[]{:S(2)}, u32[]{:S(2)}) collective-permute-start(bf16[256,128]{1,0:T(8,128)(2,1)S(1)} %shard_map.110.first), channel_id=1, source_target_pairs={{0,1},{1,0},{2,3},{3,2},{4,5},{5,4},{6,7},{7,6},{8,9},{9,8},{10,11... | collective-permute-start | bytes 196616 | tf_op jit(solution)/shard_map/ppermute | solution.py:341
  50.7 2.1 %collective-permute-done.12.three = bf16[256,128]{1,0:T(8,128)(2,1)S(1)} collective-permute-done((bf16[256,128]{1,0:T(8,128)(2,1)S(1)}, bf16[256,128]{1,0:T(8,128)(2,1)S(1)}, u32[]{:S(2)}, u32[]{:S(2)}) %collective-permute-start.12) | collective-permute-done | bytes 65568 | tf_op jit(solution)/shard_map/ppermute | solution.py:341
  52.7 1.3 %collective-permute-done.10.one = bf16[256,128]{1,0:T(8,128)(2,1)S(1)} collective-permute-done((bf16[256,128]{1,0:T(8,128)(2,1)S(1)}, bf16[256,128]{1,0:T(8,128)(2,1)S(1)}, u32[]{:S(2)}, u32[]{:S(2)}) %collective-permute-start.10) | collective-permute-done | bytes 65568 | tf_op jit(solution)/shard_map/ppermute | solution.py:341
  54.1 4.8 %collective-permute-start.13 = (bf16[256,128]{1,0:T(8,128)(2,1)S(1)}, bf16[256,128]{1,0:T(8,128)(2,1)S(1)}, u32[]{:S(2)}, u32[]{:S(2)}) collective-permute-start(bf16[256,128]{1,0:T(8,128)(2,1)S(1)} %shard_map.111.mine), channel_id=1, source_target_pairs={{0,4},{1,5},{2,6},{3,7},{4,0},{5,1},{6,2},{7,3},{8,12},{9,13},{10,... | collective-permute-start | bytes 196616 | tf_op jit(solution)/shard_map/ppermute | solution.py:341
  58.9 1.9 %collective-permute-start.14 = (bf16[3,32,192]{2,1,0:T(8,128)(2,1)S(1)}, bf16[3,32,192]{2,1,0:T(8,128)(2,1)S(1)}, u32[]{:S(2)}, u32[]{:S(2)}) collective-permute-start(bf16[3,32,192]{2,1,0:T(8,128)(2,1)S(1)} %get-tuple-element.78), channel_id=1, source_target_pairs={{0,8},{8,16},{16,24},{24,32},{32,40},{40,48},{48,56},{56,64},{64,7... | collective-permute-start | bytes 110600 | tf_op jit(solution)/shard_map/ppermute | solution.py:347
  60.8 3.5 %collective-permute-done.14.got_x = bf16[3,32,192]{2,1,0:T(8,128)(2,1)S(1)} collective-permute-done((bf16[3,32,192]{2,1,0:T(8,128)(2,1)S(1)}, bf16[3,32,192]{2,1,0:T(8,128)(2,1)S(1)}, u32[]{:S(2)}, u32[]{:S(2)}) %collective-permute-start.14) | collective-permute-done | bytes 36896 | tf_op jit(solution)/shard_map/ppermute | solution.py:347
  64.3 1.9 %collective-permute-start.15 = (bf16[3,16,192]{2,1,0:T(8,128)(2,1)S(1)}, bf16[3,16,192]{2,1,0:T(8,128)(2,1)S(1)}, u32[]{:S(2)}, u32[]{:S(2)}) collective-permute-start(bf16[3,16,192]{2,1,0:T(8,128)(2,1)S(1)} %shard_map.112), channel_id=1, source_target_pairs={{0,1},{1,2},{2,3},{3,4},{4,5},{5,6},{6,7},{8,9},{9,10},{10,11},{11... | collective-permute-start | bytes 55304 | tf_op jit(solution)/shard_map/ppermute | solution.py:347
  66.3 9.8 %collective-permute-done.15.got_y = bf16[3,16,192]{2,1,0:T(8,128)(2,1)S(1)} collective-permute-done((bf16[3,16,192]{2,1,0:T(8,128)(2,1)S(1)}, bf16[3,16,192]{2,1,0:T(8,128)(2,1)S(1)}, u32[]{:S(2)}, u32[]{:S(2)}) %collective-permute-start.15) | collective-permute-done | bytes 18464 | tf_op jit(solution)/shard_map/ppermute | solution.py:347
  76.1 1.5 %shard_map.113 = bf16[1,1,3,64,192]{4,3,2,1,0:T(8,128)(2,1)} custom-call(s32[1,1,3]{2,1,0:T(1,128)} %valid_in.7, f32[3,64,192]{2,1,0:T(8,128)S(1)} %get-tuple-element.77.local, bf16[3,32,192]{2,1,0:T(8,128)(2,1)S(1)} %collective-permute-done.14.got_x, bf16[3,16,192]{2,1,0:T(8,128)(2,1)S(1)} %collective-permute-done.15.got_y), custom_call_target="tpu_custom_call" | custom-call | bytes 202764 | tf_op jit(solution)/shard_map/pallas_call | solution.py:39
  77.6 0.8 shard_map.114
  (12 shorter events, 0.2 us)
Async XLA Ops:
  1.6 14.0 %collective-permute-start.2 = (bf16[3,8,192]{2,1,0:T(8,128)(2,1)S(1)}, bf16[3,8,192]{2,1,0:T(8,128)(2,1)S(1)}, u32[]{:S(2)}, u32[]{:S(2)}) collective-permute-start(bf16[3,8,192]{2,1,0:T(8,128)(2,1)S(1)} %get-tuple-element.43), channel_id=1, source_target_pairs={{9,0},{10,1},{11,2},{12,3},{13,4},{14,5},{15,6},{17,8},{18,9},{19,... | collective-permute-start | bytes 27656 | tf_op jit(solution)/shard_map/ppermute | solution.py:423
  5.3 10.3 %collective-permute-start = (bf16[3,16,192]{2,1,0:T(8,128)(2,1)S(1)}, bf16[3,16,192]{2,1,0:T(8,128)(2,1)S(1)}, u32[]{:S(2)}, u32[]{:S(2)}) collective-permute-start(bf16[3,16,192]{2,1,0:T(8,128)(2,1)S(1)} %get-tuple-element.52), channel_id=1, source_target_pairs={{8,0},{16,8},{24,16},{32,24},{40,32},{48,40},{56,48},{64,56},{72,6... | collective-permute-start | bytes 55304 | tf_op jit(solution)/shard_map/ppermute | solution.py:347
  8.9 6.7 %collective-permute-start.1 = (bf16[3,16,192]{2,1,0:T(8,128)(2,1)S(1)}, bf16[3,16,192]{2,1,0:T(8,128)(2,1)S(1)}, u32[]{:S(2)}, u32[]{:S(2)}) collective-permute-start(bf16[3,16,192]{2,1,0:T(8,128)(2,1)S(1)} %get-tuple-element.53), channel_id=1, source_target_pairs={{1,0},{2,1},{3,2},{4,3},{5,4},{6,5},{7,6},{9,8},{10,9},{11,10},{12... | collective-permute-start | bytes 55304 | tf_op jit(solution)/shard_map/ppermute | solution.py:347
  18.2 2.7 %collective-permute-start.3 = (bf16[4096,128]{1,0:T(8,128)(2,1)S(1)}, bf16[4096,128]{1,0:T(8,128)(2,1)S(1)}, u32[]{:S(2)}, u32[]{:S(2)}) collective-permute-start(bf16[4096,128]{1,0:T(8,128)(2,1)S(1)} %get-tuple-element.55), channel_id=1, source_target_pairs={{0,8},{8,0},{16,24},{24,16},{32,40},{40,32},{48,56},{56,48},{64,72... | collective-permute-start | bytes 3145736 | tf_op jit(solution)/shard_map/ppermute | solution.py:341
  21.2 8.1 %collective-permute-start.4 = (bf16[1024,128]{1,0:T(8,128)(2,1)S(1)}, bf16[1024,128]{1,0:T(8,128)(2,1)S(1)}, u32[]{:S(2)}, u32[]{:S(2)}) collective-permute-start(bf16[1024,128]{1,0:T(8,128)(2,1)S(1)} %get-tuple-element.62), channel_id=1, source_target_pairs={{0,64},{8,24},{16,80},{24,8},{32,96},{40,56},{48,112},{56,40},{64,... | collective-permute-start | bytes 786440 | tf_op jit(solution)/shard_map/ppermute | solution.py:386
  22.8 10.2 %collective-permute-start.5 = (bf16[1024,128]{1,0:T(8,128)(2,1)S(1)}, bf16[1024,128]{1,0:T(8,128)(2,1)S(1)}, u32[]{:S(2)}, u32[]{:S(2)}) collective-permute-start(bf16[1024,128]{1,0:T(8,128)(2,1)S(1)} %get-tuple-element.63), channel_id=1, source_target_pairs={{0,128},{8,40},{16,144},{24,56},{32,160},{40,8},{48,176},{56,24},{... | collective-permute-start | bytes 786440 | tf_op jit(solution)/shard_map/ppermute | solution.py:386
  25.8 10.0 %collective-permute-start.6 = (bf16[1024,128]{1,0:T(8,128)(2,1)S(1)}, bf16[1024,128]{1,0:T(8,128)(2,1)S(1)}, u32[]{:S(2)}, u32[]{:S(2)}) collective-permute-start(bf16[1024,128]{1,0:T(8,128)(2,1)S(1)} %get-tuple-element.64), channel_id=1, source_target_pairs={{0,192},{8,56},{16,208},{24,40},{32,224},{40,24},{48,240},{56,8},{... | collective-permute-start | bytes 786440 | tf_op jit(solution)/shard_map/ppermute | solution.py:386
  35.8 4.5 %collective-permute-start.7 = (bf16[256,128]{1,0:T(8,128)(2,1)S(1)}, bf16[256,128]{1,0:T(8,128)(2,1)S(1)}, u32[]{:S(2)}, u32[]{:S(2)}) collective-permute-start(bf16[256,128]{1,0:T(8,128)(2,1)S(1)} %get-tuple-element.70), channel_id=1, source_target_pairs={{0,16},{8,72},{16,0},{24,88},{32,48},{40,104},{48,32},{56,120},{64... | collective-permute-start | bytes 196616 | tf_op jit(solution)/shard_map/ppermute | solution.py:386
  36.0 7.3 %collective-permute-start.8 = (bf16[256,128]{1,0:T(8,128)(2,1)S(1)}, bf16[256,128]{1,0:T(8,128)(2,1)S(1)}, u32[]{:S(2)}, u32[]{:S(2)}) collective-permute-start(bf16[256,128]{1,0:T(8,128)(2,1)S(1)} %get-tuple-element.71), channel_id=1, source_target_pairs={{0,32},{8,136},{16,48},{24,152},{32,0},{40,168},{48,16},{56,184},{... | collective-permute-start | bytes 196616 | tf_op jit(solution)/shard_map/ppermute | solution.py:386
  40.4 6.1 %collective-permute-start.9 = (bf16[256,128]{1,0:T(8,128)(2,1)S(1)}, bf16[256,128]{1,0:T(8,128)(2,1)S(1)}, u32[]{:S(2)}, u32[]{:S(2)}) collective-permute-start(bf16[256,128]{1,0:T(8,128)(2,1)S(1)} %get-tuple-element.72), channel_id=1, source_target_pairs={{0,48},{8,200},{16,32},{24,216},{32,16},{40,232},{48,0},{56,248},{... | collective-permute-start | bytes 196616 | tf_op jit(solution)/shard_map/ppermute | solution.py:386
  46.5 6.3 %collective-permute-start.12 = (bf16[256,128]{1,0:T(8,128)(2,1)S(1)}, bf16[256,128]{1,0:T(8,128)(2,1)S(1)}, u32[]{:S(2)}, u32[]{:S(2)}) collective-permute-start(bf16[256,128]{1,0:T(8,128)(2,1)S(1)} %shard_map.110.first), channel_id=1, source_target_pairs={{0,3},{1,2},{2,1},{3,0},{4,7},{5,6},{6,5},{7,4},{8,11},{9,10},{10,... | collective-permute-start | bytes 196616 | tf_op jit(solution)/shard_map/ppermute | solution.py:341
  46.6 6.2 %collective-permute-start.11 = (bf16[256,128]{1,0:T(8,128)(2,1)S(1)}, bf16[256,128]{1,0:T(8,128)(2,1)S(1)}, u32[]{:S(2)}, u32[]{:S(2)}) collective-permute-start(bf16[256,128]{1,0:T(8,128)(2,1)S(1)} %shard_map.110.first), channel_id=1, source_target_pairs={{0,2},{1,3},{2,0},{3,1},{4,6},{5,7},{6,4},{7,5},{8,10},{9,11},{10,... | collective-permute-start | bytes 196616 | tf_op jit(solution)/shard_map/ppermute | solution.py:341
  49.8 4.3 %collective-permute-start.10 = (bf16[256,128]{1,0:T(8,128)(2,1)S(1)}, bf16[256,128]{1,0:T(8,128)(2,1)S(1)}, u32[]{:S(2)}, u32[]{:S(2)}) collective-permute-start(bf16[256,128]{1,0:T(8,128)(2,1)S(1)} %shard_map.110.first), channel_id=1, source_target_pairs={{0,1},{1,0},{2,3},{3,2},{4,5},{5,4},{6,7},{7,6},{8,9},{9,8},{10,11... | collective-permute-start | bytes 196616 | tf_op jit(solution)/shard_map/ppermute | solution.py:341
  54.1 23.5 %collective-permute-start.13 = (bf16[256,128]{1,0:T(8,128)(2,1)S(1)}, bf16[256,128]{1,0:T(8,128)(2,1)S(1)}, u32[]{:S(2)}, u32[]{:S(2)}) collective-permute-start(bf16[256,128]{1,0:T(8,128)(2,1)S(1)} %shard_map.111.mine), channel_id=1, source_target_pairs={{0,4},{1,5},{2,6},{3,7},{4,0},{5,1},{6,2},{7,3},{8,12},{9,13},{10,... | collective-permute-start | bytes 196616 | tf_op jit(solution)/shard_map/ppermute | solution.py:341
  58.9 5.4 %collective-permute-start.14 = (bf16[3,32,192]{2,1,0:T(8,128)(2,1)S(1)}, bf16[3,32,192]{2,1,0:T(8,128)(2,1)S(1)}, u32[]{:S(2)}, u32[]{:S(2)}) collective-permute-start(bf16[3,32,192]{2,1,0:T(8,128)(2,1)S(1)} %get-tuple-element.78), channel_id=1, source_target_pairs={{0,8},{8,16},{16,24},{24,32},{32,40},{40,48},{48,56},{56,64},{64,7... | collective-permute-start | bytes 110600 | tf_op jit(solution)/shard_map/ppermute | solution.py:347
  64.3 11.7 %collective-permute-start.15 = (bf16[3,16,192]{2,1,0:T(8,128)(2,1)S(1)}, bf16[3,16,192]{2,1,0:T(8,128)(2,1)S(1)}, u32[]{:S(2)}, u32[]{:S(2)}) collective-permute-start(bf16[3,16,192]{2,1,0:T(8,128)(2,1)S(1)} %shard_map.112), channel_id=1, source_target_pairs={{0,1},{1,2},{2,3},{3,4},{4,5},{5,6},{6,7},{8,9},{9,10},{10,11},{11... | collective-permute-start | bytes 55304 | tf_op jit(solution)/shard_map/ppermute | solution.py:347
